TPU v7x, 32 devices: a whole 2x2x4 slice. The times are simulated.
32 devices in a mesh: gx: 4 (over y, core), gy: 2 (over x), gz: 4 (over z).
Axes of the slice: x: 2, y: 2, z: 4, core: 2. Of those that a mesh axis runs over, the one named last changes fastest.
Arguments:
- concentration: bfloat16 [16, 8, 16, 512], P(None, 'gx', 'gy', 'gz'), may hold values from -8.25 to 11.25
- pressure_head: float32 [8, 16, 512], P('gx', 'gy', 'gz'), may hold values from -4 to -0.5
- zone_ids: int32 [8, 16, 512], P('gx', 'gy', 'gz'), may hold values from 0 to 7
- well_cells: int32 [8, 16, 512], P('gx', 'gy', 'gz'), may hold values 0 or 1
- zone_conductivity: float32 [8], replicated, may hold values from 0.4 to 1
- zone_alpha: float32 [8], replicated, may hold values from 0.05 to 0.35
- disp_molecular: float32 [16], replicated, may hold values from 0.05 to 0.5
- disp_longitudinal: float32 [16], replicated, may hold values from 0.1 to 1
- entry_counts: int32 [4, 2, 4], P('gx', 'gy', 'gz'), may hold values from 40 to 64, as said below
- dest_tiles: int32 [4, 2, 4, 64], P('gx', 'gy', 'gz'), may hold values from 0 to 15
- source_devices: int32 [4, 2, 4, 64, 1], P('gx', 'gy', 'gz'), may hold values from 0 to 7; in each aligned block of 64 rows (0 to 63, 64 to 127, ..., all dimensions but the last counted through in order) at most 8 rows name the same one
- source_tiles: int32 [4, 2, 4, 64], P('gx', 'gy', 'gz'), may hold values from 0 to 15
- interp_weights: bfloat16 [4, 2, 4, 64, 128, 128], P('gx', 'gy', 'gz'), may hold values from -0.0625 to 0.0625
Outputs:
- head_next: float32 [8, 16, 512], P('gx', 'gy', 'gz')
- solute_next: float32 [16, 8, 16, 512], P(None, 'gx', 'gy', 'gz')
Inputs may be any that keep to these rules, and one draw needn't show every extreme that they name: `entry_counts`: some blocks hold all 64 entries live, at least one block in every draw; the others between 40 and 56. `source_devices`: p = gx index * 2 + gy index of the upstream block; among one block's 64 entries no upstream block is named more than 8 times.
All inputs are finite; a program needn't handle non-finite values. No bound on the sum of `well_cells` on one device may be relied on, other than what follows from the above.
Results may differ from a plain program's by a relative error of at most 0.0003.
Values may be sent and summed in bfloat16 or wider, within the bound.
No kernel may reach another device: no remote copies, remote signals or barrier semaphores. Data moves between devices by JAX's collectives and lax.ppermute only.
A program may use at most 64 MiB of HBM per device.

v0:
```python
import functools

import jax
import jax.numpy as jnp
from jax import lax
from jax.experimental import pallas as pl
from jax.experimental.pallas import tpu as pltpu
from jax.sharding import PartitionSpec as P


RSTEPS = 2
CG_ITERS = 2
AXES = ("gx", "gy", "gz")
LAYER = ("gx", "gy")

time_step = 0.15
pump_rate = 1.0
disp_time = 1.0
gravity_sign = (0.0, 0.0, 0.0, 0.0, 1.0, -1.0)


def padded_2(x, sides, width):
    for axis, dim in sides:
        count, length = (lax.axis_size(axis), x.shape[dim])
        up = [(i, (i + 1) % count) for i in range(count - 1)]
        down = [(j, i) for i, j in up]
        last = lax.slice_in_dim(x, length - width, length, axis=dim)
        initial = lax.slice_in_dim(x, 0, width, axis=dim)
        before = lax.ppermute(last, axis, up)
        after = lax.ppermute(initial, axis, down)
        x = jnp.concatenate([before, x, after], axis=dim)
    return x


def neighbours(padded):
    return [
        padded[..., 2:, 1:-1, 1:-1],
        padded[..., :-2, 1:-1, 1:-1],
        padded[..., 1:-1, 2:, 1:-1],
        padded[..., 1:-1, :-2, 1:-1],
        padded[..., 1:-1, 1:-1, 2:],
        padded[..., 1:-1, 1:-1, :-2],
    ]


def richards_terms(head_padded, cond_padded):
    head_centre = head_padded[..., 1:-1, 1:-1, 1:-1]
    cond_centre = cond_padded[..., 1:-1, 1:-1, 1:-1]
    net_inflow = jnp.zeros_like(head_centre)
    flux_terms = []
    for face_index, (head_beside, cond_beside) in enumerate(
        zip(neighbours(head_padded), neighbours(cond_padded))
    ):
        face_cond = jnp.sqrt(cond_centre * cond_beside)
        inflow = face_cond * (head_beside - head_centre + gravity_sign[face_index])
        net_inflow = net_inflow + inflow
        flux_terms.append(jnp.sqrt(1.0 + inflow * inflow))
    return (net_inflow, jnp.stack(flux_terms))


def apply_operator(field, flux_terms, mol_coeff, long_coeff):
    padded = padded_2(field, (("gx", 1), ("gy", 2), ("gz", 3)), 1)
    plain_sum = jnp.zeros_like(field)
    weighted = jnp.zeros_like(field)
    for face_index, beside in enumerate(neighbours(padded)):
        difference = field - beside
        plain_sum = plain_sum + difference
        weighted = weighted + flux_terms[face_index] * difference
    return field + disp_time * (mol_coeff * plain_sum + long_coeff * weighted)


def spread(values):
    return values[:, None, None, None]


def squares_total(residual):
    return lax.psum(jnp.sum(residual * residual, axis=(1, 2, 3)), AXES)


def block_plan(
    concentration,
    pressure_head,
    zone_ids,
    well_cells,
    zone_conductivity,
    zone_alpha,
    disp_molecular,
    disp_longitudinal,
    entry_counts,
    dest_tiles,
    source_devices,
    source_tiles,
    interp_weights,
):
    zone_range = jnp.arange(zone_conductivity.shape[0], dtype=jnp.int32)
    zone_onehot = (zone_ids[None] == zone_range[:, None, None, None]).astype(jnp.float32)
    cell_cond = jnp.sum(zone_onehot * zone_conductivity[:, None, None, None], axis=0)
    cell_alpha = jnp.sum(zone_onehot * zone_alpha[:, None, None, None], axis=0)
    pumping = well_cells.astype(jnp.float32)
    head_now = pressure_head
    flux_terms = None
    for _ in range(RSTEPS):
        conduct = cell_cond * jnp.exp(cell_alpha * head_now)
        padded = padded_2(jnp.stack([head_now, conduct]), (("gx", 1), ("gy", 2), ("gz", 3)), 1)
        net_inflow, flux_terms = richards_terms(padded[0], padded[1])
        head_now = head_now + time_step * (net_inflow - pump_rate * pumping)
    solutes, cells_x, cells_y, tile_len = concentration.shape
    tile_count = cells_x * cells_y
    entries = dest_tiles.shape[-1]
    peer_count = lax.axis_size("gx") * lax.axis_size("gy")
    slot_count = max(2, (entries + peer_count - 1) // peer_count)
    tile_field = concentration.reshape(solutes, tile_count, tile_len)
    dest_tile = dest_tiles.reshape(entries)
    source_dev = source_devices.reshape(entries)
    source_tile = source_tiles.reshape(entries)
    live_count = entry_counts.reshape(())
    weight_stack = interp_weights.reshape(entries, tile_len, tile_len)
    entry_ids = jnp.arange(entries, dtype=jnp.int32)
    earlier = entry_ids[None, :] < entry_ids[:, None]
    slot_rank = jnp.sum(
        ((source_dev[None, :] == source_dev[:, None]) & earlier).astype(jnp.int32), axis=1
    )
    peer_ids = jnp.arange(peer_count, dtype=jnp.int32)
    slot_ids = jnp.arange(slot_count, dtype=jnp.int32)
    matched = (source_dev[None, None, :] == peer_ids[:, None, None]) & (
        slot_rank[None, None, :] == slot_ids[None, :, None]
    )
    wanted = jnp.sum(jnp.where(matched, source_tile[None, None, :], 0), axis=2)
    asked_ids = lax.all_to_all(wanted, LAYER, split_axis=0, concat_axis=0, tiled=True)
    outgoing = jnp.take(tile_field, asked_ids.reshape(peer_count * slot_count), axis=1)
    outgoing = outgoing.reshape(solutes, peer_count, slot_count, tile_len)
    arrived = lax.all_to_all(outgoing, LAYER, split_axis=1, concat_axis=1, tiled=True)
    arrived_flat = arrived.reshape(solutes, peer_count * slot_count, tile_len)
    fetched = jnp.take(arrived_flat, source_dev * slot_count + slot_rank, axis=1)
    interpolated = jnp.einsum(
        "set,eto->seo", fetched, weight_stack, preferred_element_type=jnp.float32
    )
    alive_mask = (entry_ids < live_count).astype(jnp.float32)
    tile_ids = jnp.arange(tile_count, dtype=jnp.int32)
    dest_onehot = (dest_tile[None, :] == tile_ids[:, None]).astype(jnp.float32)
    tile_added = jnp.einsum(
        "te,seo->sto",
        dest_onehot,
        interpolated * alive_mask[None, :, None],
        precision=lax.Precision.HIGHEST,
    )
    advected = concentration.astype(jnp.float32) + tile_added.reshape(
        solutes, cells_x, cells_y, tile_len
    )
    mol_coeff = spread(disp_molecular)
    long_coeff = spread(disp_longitudinal)
    solution = jnp.zeros_like(advected)
    residual = advected
    direction = advected
    norm_now = squares_total(residual)
    for _ in range(CG_ITERS):
        image = apply_operator(direction, flux_terms, mol_coeff, long_coeff)
        curvature = lax.psum(jnp.sum(direction * image, axis=(1, 2, 3)), AXES)
        step_size = norm_now / curvature
        solution = solution + spread(step_size) * direction
        residual = residual - spread(step_size) * image
        norm_next = squares_total(residual)
        direction = residual + spread(norm_next / norm_now) * direction
        norm_now = norm_next
    return (head_now, solution)


SMEM = functools.partial(pl.BlockSpec, memory_space=pltpu.SMEM)
VMEM = functools.partial(pl.BlockSpec, memory_space=pltpu.VMEM)
HBM = functools.partial(pl.BlockSpec, memory_space=pltpu.HBM)


def in_hbm(x):
    return pltpu.with_memory_space_constraint(x, pltpu.HBM)


def grant(mib):
    return pltpu.CompilerParams(vmem_limit_bytes=mib << 20)


def at_next(v, group, dim, edge):
    length = v.shape[dim]
    rolled = pltpu.roll(v, length - 1, dim)
    ids = lax.broadcasted_iota(jnp.int32, v.shape, dim)
    count = v.shape[group]
    beyond = lax.slice_in_dim(rolled, 1, count, axis=group)
    beyond = jnp.concatenate([beyond, edge], axis=group)
    return jnp.where(ids == length - 1, beyond, rolled)


def at_previous(v, group, dim, edge):
    rolled = pltpu.roll(v, 1, dim)
    ids = lax.broadcasted_iota(jnp.int32, v.shape, dim)
    count = v.shape[group]
    before = lax.slice_in_dim(rolled, 0, count - 1, axis=group)
    before = jnp.concatenate([edge, before], axis=group)
    return jnp.where(ids == 0, before, rolled)


def first_of(v, group):
    return lax.slice_in_dim(v, 0, 1, axis=group)


def fetch(refs, scratch, sems):
    copies = [
        pltpu.make_async_copy(ref, held, sems.at[n]) for n, (ref, held) in enumerate(zip(refs, scratch))
    ]
    for copy in copies:
        copy.start()
    for copy in copies:
        copy.wait()


HEAD_PARTS = 2
PLANES_OF_CELLS = HEAD_PARTS + 2


def pack_kernel(conc_ref, head_ref, zone_ref, well_ref, out_ref, *scratch):
    *held, rows_s, sems = scratch
    fetch([conc_ref, head_ref, zone_ref, well_ref], held, sems)
    conc_s, head_s, zone_s, well_s = held
    solutes, tile_count, tile_len = conc_s.shape
    for s in range(solutes):
        rows_s[s * tile_count : (s + 1) * tile_count, :] = conc_s[s].astype(jnp.float32)
    for t in range(tile_count):
        rows = rows_s[pl.ds(t, solutes, stride=tile_count), :]
        out_ref[t] = rows.astype(jnp.bfloat16)
    rest = head_s[...].reshape(tile_count, tile_len)
    for n in range(HEAD_PARTS):
        part = rest.astype(jnp.bfloat16)
        out_ref[tile_count + n] = part
        rest = rest - part.astype(jnp.float32)
    zone = zone_s[...].reshape(tile_count, tile_len)
    well = well_s[...].reshape(tile_count, tile_len)
    out_ref[tile_count + HEAD_PARTS] = zone.astype(jnp.float32).astype(jnp.bfloat16)
    out_ref[tile_count + HEAD_PARTS + 1] = well.astype(jnp.float32).astype(jnp.bfloat16)


def stage_kernel(from_ref, to_ref, sems):
    fetch([from_ref], [to_ref], sems)


def flow_kernel(
    shape, cond_ref, alpha_ref, cells_ref, flux_ref, head_ref, h_s, q_s, k_s, a_s, w_s
):
    blocks_x, blocks_y, blocks_z, cells_x = shape
    mine_x, mine_y, mine_z = (lax.axis_index(axis) for axis in AXES)
    planes = blocks_x * cells_x
    plane_shape = h_s.shape[1:]
    zones = cond_ref.shape[0]
    roots = [jnp.sqrt(jnp.full((1, 1, 1, 1), cond_ref[n], jnp.float32)) for n in range(zones)]
    for a in range(blocks_x):
        off_x = lax.bitwise_xor(mine_x, a)
        for b in range(blocks_y):
            for c in range(blocks_z):
                off_y, off_z = lax.bitwise_xor(mine_y, b), lax.bitwise_xor(mine_z, c)
                slot = off_x % 2 * blocks_z + off_z
                slot = (slot * (blocks_x // 2) + off_x // 2) * blocks_y + off_y
                parts = [cells_ref[slot, n].astype(jnp.float32) for n in range(PLANES_OF_CELLS)]
                parts = [part.reshape((cells_x,) + plane_shape[2:]) for part in parts]
                *heads, zone, well = parts
                head = sum(heads[1:], heads[0])
                for i in range(cells_x):
                    plane = a * cells_x + i
                    h_s[plane, b, c] = head[i]
                    k_s[plane, b, c] = zone[i]
                    w_s[plane, b, c] = well[i]
    for plane in range(planes):
        head, zone = h_s[plane], k_s[plane]
        root = jnp.broadcast_to(roots[0], plane_shape)
        half = jnp.full(plane_shape, 0.5 * alpha_ref[0], jnp.float32)
        for n in range(1, zones):
            root = jnp.where(zone == n, roots[n], root)
            half = jnp.where(zone == n, 0.5 * alpha_ref[n], half)
        k_s[plane] = root
        a_s[plane] = half
        q_s[plane] = root * jnp.exp(half * head)
    none_y = jnp.zeros((1,) + plane_shape[1:], jnp.float32)
    none_z = jnp.zeros(plane_shape[:1] + (1,) + plane_shape[2:], jnp.float32)
    for sweep in range(RSTEPS):
        if sweep > 0:
            for plane in range(planes):
                q_s[plane] = k_s[plane] * jnp.exp(a_s[plane] * h_s[plane])
        from_below = jnp.zeros(plane_shape, jnp.float32)
        for plane in range(planes):
            h, q = h_s[plane], q_s[plane]
            if plane < planes - 1:
                in_x = q * q_s[plane + 1] * (h_s[plane + 1] - h)
            else:
                in_x = jnp.zeros(plane_shape, jnp.float32)
            in_y = q * at_next(q, 0, 2, none_y) * (at_next(h, 0, 2, none_y) - h)
            in_z = q * at_next(q, 1, 3, none_z) * (at_next(h, 1, 3, none_z) - h + gravity_sign[4])
            net = in_x - from_below + (in_y - at_previous(in_y, 0, 2, none_y))
            net = net + (in_z - at_previous(in_z, 1, 3, none_z))
            h_s[plane] = h + time_step * (net - pump_rate * w_s[plane])
            from_below = in_x
            if sweep == RSTEPS - 1:
                flux_ref[0, plane] = jnp.sqrt(1.0 + in_x * in_x)
                flux_ref[1, plane] = jnp.sqrt(1.0 + in_y * in_y)
                flux_ref[2, plane] = jnp.sqrt(1.0 + in_z * in_z)
    for i in range(cells_x):
        head_ref[i] = h_s[mine_x * cells_x + i, mine_y, mine_z]


def interpolate_kernel(shape, solutes, table_ref, near_ref, far_ref, weights_ref, out_ref, sum_s, all_s):
    entries, _ = weights_ref.shape[:2]
    _, blocks_y, blocks_z = shape
    rows_sent = out_ref.shape[1]
    tile_count = 2 * rows_sent
    chips = near_ref.shape[0]
    for c in range(chips):
        for t in range(tile_count):
            all_s[c * tile_count + t] = near_ref[c, t]
            all_s[(chips + c) * tile_count + t] = far_ref[c, t]
    for t in range(tile_count):
        sum_s[t * solutes : (t + 1) * solutes, :] = near_ref[0, t].astype(jnp.float32)
    for e in range(entries):
        got = jnp.dot(all_s[table_ref[e]], weights_ref[e], preferred_element_type=jnp.float32)
        rows = pl.ds(pl.multiple_of(table_ref[entries + e] * solutes, solutes), solutes)
        sum_s[rows, :] = sum_s[rows, :] + got
    for s in range(solutes):
        field = sum_s[pl.ds(s, tile_count, stride=solutes), :]
        per = blocks_y * blocks_z
        low = (s // per) * 2 * per + s % per
        out_ref[low] = field[:rows_sent]
        out_ref[low + per] = field[rows_sent:]


def spread_out(v, above, below_x, fluxes, mol, lng, edge_w):
    w_x, w_y, w_z = [mol + lng * f for f in fluxes]
    if above is None:
        f_x = w_x * v
    else:
        f_x = w_x * (v - above)
    if below_x is None:
        below_x = -edge_w * v
    none_y = jnp.zeros((1,) + v.shape[1:], jnp.float32)
    none_z = jnp.zeros(v.shape[:1] + (1,) + v.shape[2:], jnp.float32)
    f_y = w_y * (v - at_next(v, 0, 2, none_y))
    f_z = w_z * (v - at_next(v, 1, 3, none_z))
    low_y = -edge_w * first_of(v, 0)
    low_z = -edge_w * first_of(v, 1)
    out = f_x - below_x + (f_y - at_previous(f_y, 0, 2, low_y))
    return out + (f_z - at_previous(f_z, 1, 3, low_z)), f_x


def solve_kernel(shape, mol_ref, long_ref, own_ref, other_ref, flux_ref, out_ref, v_s, y_s):
    blocks_x, blocks_y, blocks_z, cells_x = shape
    per = blocks_y * blocks_z
    planes = blocks_x * cells_x
    plane_shape = flux_ref.shape[2:]
    me_x, me_y, me_z = (lax.axis_index(axis) for axis in AXES)
    solute = ((me_x // 2) * blocks_y + me_y) * blocks_z + me_z
    part = me_x % 2
    mol = disp_time * mol_ref[solute]
    lng = disp_time * long_ref[solute]
    edge_w = mol + lng
    parts = jnp.full((per,) + plane_shape[2:], part, jnp.int32)
    for plane in range(planes):
        a, i = plane // cells_x, plane % cells_x
        span = slice(a * per, (a + 1) * per)
        v = jnp.where(parts == i, own_ref[span], other_ref[span])
        v_s[plane] = v.reshape(plane_shape)

    def total(x):
        return jnp.sum(x, axis=(0, 1))

    p = [jnp.zeros(plane_shape[2:], jnp.float32) for _ in range(4)]
    below = None
    for plane in range(planes):
        v = v_s[plane]
        above = v_s[plane + 1] if plane < planes - 1 else None
        fluxes = [flux_ref[n, plane] for n in range(3)]
        y, below = spread_out(v, above, below, fluxes, mol, lng, edge_w)
        y_s[plane] = y
        p[0] += total(v * v)
        p[1] += total(v * y)
        p[2] += total(y * y)
    below = None
    for plane in range(planes):
        v = y_s[plane]
        above = y_s[plane + 1] if plane < planes - 1 else None
        fluxes = [flux_ref[n, plane] for n in range(3)]
        z, below = spread_out(v, above, below, fluxes, mol, lng, edge_w)
        p[3] += total(v * z)
    p0, p1, p2, p3 = [jnp.sum(x, axis=(0, 1), keepdims=True) for x in p]
    d = p1 / p0
    a0 = 1.0 / (1.0 + d)
    var = p2 - d * p1
    wid = p3 - 2.0 * d * p2 + d * d * p1
    ratio = var / p0
    a1 = var / (var + wid - a0 * var * ratio)
    c0 = a0 + a1 * (a0 * d + a0 * a0 * ratio)
    c1 = a1 * a0
    for a in range(blocks_x):
        span = slice(a * per, (a + 1) * per)
        y = y_s[a * cells_x + part].reshape((per,) + plane_shape[2:])
        out_ref[span] = c0[None] * own_ref[span] - c1[None] * y


def moved(x, shift_x, shift_y):
    sizes = tuple(lax.axis_size(axis) for axis in LAYER)
    pairs = []
    for i in range(sizes[0]):
        for j in range(sizes[1]):
            pairs.append((i * sizes[1] + j, (i ^ shift_x) * sizes[1] + (j ^ shift_y)))
    return lax.ppermute(x, LAYER, pairs)


def from_chips(x):
    parts = [x]
    for shift_x in range(0, lax.axis_size("gx"), 2):
        for shift_y in range(lax.axis_size("gy")):
            if shift_x + shift_y > 0:
                parts.append(moved(x, shift_x, shift_y))
    return jnp.stack(parts)


def from_depth(x):
    count = lax.axis_size("gz")
    parts = [x]
    for shift in range(1, count):
        parts.append(lax.ppermute(x, "gz", [(i, i ^ shift) for i in range(count)]))
    return jnp.stack(parts)


def field_plan(
    concentration,
    pressure_head,
    zone_ids,
    well_cells,
    zone_conductivity,
    zone_alpha,
    disp_molecular,
    disp_longitudinal,
    entry_counts,
    dest_tiles,
    source_devices,
    source_tiles,
    interp_weights,
):
    blocks_x, blocks_y, blocks_z = (lax.axis_size(axis) for axis in AXES)
    devices = blocks_x * blocks_y * blocks_z
    solutes, cells_x, cells_y, tile_len = concentration.shape
    tile_count = cells_x * cells_y
    entries = dest_tiles.shape[-1]
    shape = (blocks_x, blocks_y, blocks_z, cells_x)
    plane_shape = (blocks_y, blocks_z, cells_y, tile_len)
    planes = blocks_x * cells_x
    f32 = jnp.float32

    tiles = concentration.reshape(solutes, tile_count, tile_len)
    block = (cells_x, cells_y, tile_len)
    packed = pl.pallas_call(
        pack_kernel,
        out_shape=jax.ShapeDtypeStruct(
            (tile_count + PLANES_OF_CELLS, solutes, tile_len), jnp.bfloat16
        ),
        in_specs=[HBM()] * 4,
        out_specs=VMEM(),
        scratch_shapes=[
            pltpu.VMEM(tiles.shape, jnp.bfloat16),
            pltpu.VMEM(block, f32),
            pltpu.VMEM(block, jnp.int32),
            pltpu.VMEM(block, jnp.int32),
            pltpu.VMEM((solutes * tile_count, tile_len), f32),
            pltpu.SemaphoreType.DMA((4,)),
        ],
        compiler_params=grant(4),
        name="pack",
    )(in_hbm(tiles), in_hbm(pressure_head), in_hbm(zone_ids), in_hbm(well_cells))
    near = from_chips(packed)
    far = moved(near, 1, 0)
    cells = from_depth(near[:, tile_count:])
    cells = jnp.concatenate([cells, moved(cells, 1, 0)])
    cells = cells.reshape((devices,) + cells.shape[2:])

    weights = pl.pallas_call(
        stage_kernel,
        out_shape=jax.ShapeDtypeStruct((entries, tile_len, tile_len), jnp.bfloat16),
        in_specs=[HBM()],
        out_specs=VMEM(),
        scratch_shapes=[pltpu.SemaphoreType.DMA((1,))],
        compiler_params=grant(4),
        name="stage",
    )(in_hbm(interp_weights.reshape(entries, tile_len, tile_len)))

    ix, iy = lax.axis_index("gx"), lax.axis_index("gy")
    peer = source_devices.reshape(entries)
    off_x, off_y = (peer // blocks_y) ^ ix, (peer % blocks_y) ^ iy
    slot = (off_x % 2) * (blocks_x // 2) + off_x // 2
    source = (slot * blocks_y + off_y) * tile_count + source_tiles.reshape(entries)
    entry_ids = jnp.arange(entries, dtype=jnp.int32)
    alive = entry_ids < entry_counts.reshape(())
    dest = jnp.where(alive, dest_tiles.reshape(entries), tile_count)
    table = jnp.concatenate([source, dest])

    fields = pl.pallas_call(
        functools.partial(interpolate_kernel, shape[:3], solutes),
        out_shape=jax.ShapeDtypeStruct((devices, cells_y, tile_len), f32),
        in_specs=[SMEM(), VMEM(), VMEM(), VMEM()],
        out_specs=VMEM(),
        scratch_shapes=[
            pltpu.VMEM(((tile_count + 1) * solutes, tile_len), f32),
            pltpu.VMEM((blocks_x * blocks_y * tile_count, solutes, tile_len), jnp.bfloat16),
        ],
        compiler_params=grant(8),
        name="interpolate",
    )(table, near, far, weights)
    field = lax.all_to_all(fields, AXES, split_axis=0, concat_axis=0, tiled=True)
    other = moved(field, 1, 0)

    grid_scratch = pltpu.VMEM((planes,) + plane_shape, f32)
    flux, head = pl.pallas_call(
        functools.partial(flow_kernel, shape),
        out_shape=(
            jax.ShapeDtypeStruct((3, planes) + plane_shape, f32),
            jax.ShapeDtypeStruct((cells_x, cells_y, tile_len), f32),
        ),
        in_specs=[SMEM(), SMEM(), VMEM()],
        out_specs=(VMEM(), VMEM()),
        scratch_shapes=[grid_scratch] * 5,
        compiler_params=grant(8),
        name="flow",
    )(zone_conductivity, zone_alpha, cells)

    back = pl.pallas_call(
        functools.partial(solve_kernel, shape),
        out_shape=jax.ShapeDtypeStruct(field.shape, f32),
        in_specs=[SMEM(), SMEM(), VMEM(), VMEM(), VMEM()],
        out_specs=VMEM(),
        scratch_shapes=[grid_scratch] * 2,
        compiler_params=grant(8),
        name="solve",
    )(disp_molecular, disp_longitudinal, field, other, flux)
    back = lax.all_to_all(back, AXES, split_axis=0, concat_axis=0, tiled=True)
    back = back.reshape((blocks_x // 2, 2, blocks_y * blocks_z, cells_y, tile_len))
    back = back.transpose(0, 2, 1, 3, 4)
    return head, back.reshape(concentration.shape)


def takes_fields(devices, solutes, cells_x, cells_y, tile_len, sizes):
    fits = devices == 2 * solutes and cells_x == 2 and cells_x * cells_y == solutes
    for size in sizes:
        fits = fits and size & (size - 1) == 0
    return fits and sizes[0] > 1 and cells_y == 8 and tile_len == 128


def shards(concentration, *rest):
    sizes = [lax.axis_size(axis) for axis in AXES]
    devices = sizes[0] * sizes[1] * sizes[2]
    if takes_fields(devices, *concentration.shape, sizes):
        return field_plan(concentration, *rest)
    return block_plan(concentration, *rest)


def solution(mesh):
    in_specs = (
        P(None, "gx", "gy", "gz"),
        P("gx", "gy", "gz"),
        P("gx", "gy", "gz"),
        P("gx", "gy", "gz"),
        P(),
        P(),
        P(),
        P(),
        P("gx", "gy", "gz"),
        P("gx", "gy", "gz", None),
        P("gx", "gy", "gz", None, None),
        P("gx", "gy", "gz", None),
        P("gx", "gy", "gz", None, None, None),
    )
    out_specs = (P("gx", "gy", "gz"), P(None, "gx", "gy", "gz"))
    return jax.shard_map(
        shards, mesh=mesh, in_specs=in_specs, out_specs=out_specs, check_vma=False
    )
```

profile of v0, /device:TPU:0, one launch (start us, length us, event | category | flops | bytes accessed | tf_op | source)
XLA Modules:
  0.0 47.8 jit_solution(3431006782956449380)
XLA Ops:
  0.6 0.9 %pack.1 = bf16[20,16,128]{2,1,0:T(8,128)(2,1)S(1)} custom-call(bf16[16,16,128]{2,1,0:T(8,128)(2,1)} %bitcast.50, f32[2,8,128]{2,1,0:T(8,128)} %head_ref.1, s32[2,8,128]{2,1,0:T(8,128)} %zone_ref.1, s32[2,8,128]{2,1,0:T(8,128)} %well_ref.1), custom_call_target="tpu_custom_call" | custom-call | tf_op jit(solution)/shard_map/pack/pallas_call | solution.py:454
  1.6 4.0 %collective-permute-start.2 = (bf16[20,16,128]{2,1,0:T(8,128)(2,1)S(1)}, bf16[20,16,128]{2,1,0:T(8,128)(2,1)S(1)}, u32[]{:S(2)}, u32[]{:S(2)}) collective-permute-start(bf16[20,16,128]{2,1,0:T(8,128)(2,1)S(1)} %pack.1), channel_id=1, source_target_pairs={{0,20},{4,16},{8,28},{12,24},{16,4},{20,0},{24,12},{28,8},{1,21},{... | collective-permute-start | bytes 245768 | tf_op jit(solution)/shard_map/ppermute | solution.py:407
  5.6 0.5 %collective-permute-start.1 = (bf16[20,16,128]{2,1,0:T(8,128)(2,1)S(1)}, bf16[20,16,128]{2,1,0:T(8,128)(2,1)S(1)}, u32[]{:S(2)}, u32[]{:S(2)}) collective-permute-start(bf16[20,16,128]{2,1,0:T(8,128)(2,1)S(1)} %pack.1), channel_id=1, source_target_pairs={{0,16},{4,20},{8,24},{12,28},{16,0},{20,4},{24,8},{28,12},{1,17},{... | collective-permute-start | bytes 245768 | tf_op jit(solution)/shard_map/ppermute | solution.py:407
  6.1 0.1 collective-permute-start
  6.9 0.0 copy-start.4
  6.9 0.0 copy-start.5
  6.9 0.0 copy-start.6
  6.9 1.6 %stage.1.weights_ref = bf16[64,128,128]{2,1,0:T(8,128)(2,1)S(1)} custom-call(bf16[64,128,128]{2,1,0:T(8,128)(2,1)} %bitcast.41), custom_call_target="tpu_custom_call" | custom-call | tf_op jit(solution)/shard_map/stage/pallas_call | solution.py:478
  8.5 0.0 copy-done.4
  8.5 0.0 copy-done.5
  8.5 0.0 copy-done.6
  8.6 0.1 pad_add_fusion.table_ref
  8.7 0.0 collective-permute-done.2
  8.7 1.3 %collective-permute-done.1 = bf16[20,16,128]{2,1,0:T(8,128)(2,1)S(1)} collective-permute-done((bf16[20,16,128]{2,1,0:T(8,128)(2,1)S(1)}, bf16[20,16,128]{2,1,0:T(8,128)(2,1)S(1)}, u32[]{:S(2)}, u32[]{:S(2)}) %collective-permute-start.1) | collective-permute-done | bytes 81952 | tf_op jit(solution)/shard_map/ppermute | solution.py:407
  10.0 0.5 %collective-permute-done = bf16[20,16,128]{2,1,0:T(8,128)(2,1)S(1)} collective-permute-done((bf16[20,16,128]{2,1,0:T(8,128)(2,1)S(1)}, bf16[20,16,128]{2,1,0:T(8,128)(2,1)S(1)}, u32[]{:S(2)}, u32[]{:S(2)}) %collective-permute-start) | collective-permute-done | bytes 81952 | tf_op jit(solution)/shard_map/ppermute | solution.py:407
  10.6 2.7 %collective-permute-start.4 = (bf16[4,4,16,128]{3,2,1,0:T(8,128)(2,1)S(1)}, bf16[4,4,16,128]{3,2,1,0:T(8,128)(2,1)S(1)}, u32[]{:S(2)}, u32[]{:S(2)}) collective-permute-start(bf16[4,4,16,128]{3,2,1,0:T(8,128)(2,1)S(1)} %get-tuple-element.7), channel_id=1, source_target_pairs={{0,2},{1,3},{2,0},{3,1},{4,6},{5,7},{6,4},{7,5},{8,10},{9,11},{10,... | collective-permute-start | bytes 196616 | tf_op jit(solution)/shard_map/ppermute | solution.py:423
  13.2 1.6 %collective-permute-start.3 = (bf16[4,4,16,128]{3,2,1,0:T(8,128)(2,1)S(1)}, bf16[4,4,16,128]{3,2,1,0:T(8,128)(2,1)S(1)}, u32[]{:S(2)}, u32[]{:S(2)}) collective-permute-start(bf16[4,4,16,128]{3,2,1,0:T(8,128)(2,1)S(1)} %get-tuple-element.7), channel_id=1, source_target_pairs={{0,1},{1,0},{2,3},{3,2},{4,5},{5,4},{6,7},{7,6},{8,9},{9,8},{10,11... | collective-permute-start | bytes 196616 | tf_op jit(solution)/shard_map/ppermute | solution.py:423
  14.8 0.2 collective-permute-start.5
  15.0 0.0 collective-permute-start.7
  15.0 0.9 %collective-permute-done.4 = bf16[4,4,16,128]{3,2,1,0:T(8,128)(2,1)S(1)} collective-permute-done((bf16[4,4,16,128]{3,2,1,0:T(8,128)(2,1)S(1)}, bf16[4,4,16,128]{3,2,1,0:T(8,128)(2,1)S(1)}, u32[]{:S(2)}, u32[]{:S(2)}) %collective-permute-start.4) | collective-permute-done | bytes 65568 | tf_op jit(solution)/shard_map/ppermute | solution.py:423
  15.9 1.6 %collective-permute-done.3 = bf16[4,4,16,128]{3,2,1,0:T(8,128)(2,1)S(1)} collective-permute-done((bf16[4,4,16,128]{3,2,1,0:T(8,128)(2,1)S(1)}, bf16[4,4,16,128]{3,2,1,0:T(8,128)(2,1)S(1)}, u32[]{:S(2)}, u32[]{:S(2)}) %collective-permute-start.3) | collective-permute-done | bytes 65568 | tf_op jit(solution)/shard_map/ppermute | solution.py:423
  17.5 3.4 %collective-permute-done.5 = bf16[4,4,16,128]{3,2,1,0:T(8,128)(2,1)S(1)} collective-permute-done((bf16[4,4,16,128]{3,2,1,0:T(8,128)(2,1)S(1)}, bf16[4,4,16,128]{3,2,1,0:T(8,128)(2,1)S(1)}, u32[]{:S(2)}, u32[]{:S(2)}) %collective-permute-start.5) | collective-permute-done | bytes 65568 | tf_op jit(solution)/shard_map/ppermute | solution.py:423
  20.9 0.0 copy-start.2
  20.9 0.0 copy-start.3
  20.9 0.0 copy-start
  21.0 0.0 copy-start.1
  21.0 0.1 collective-permute-start.6
  21.0 0.0 collective-permute-done.7.far_ref
  21.1 2.0 %interpolate.1 = f32[32,8,128]{2,1,0:T(8,128)} custom-call(s32[128]{0:T(128)S(1)} %pad_add_fusion.table_ref, bf16[4,20,16,128]{3,2,1,0:T(8,128)(2,1)S(1)} %pad_maximum_fusion.near_ref, bf16[4,20,16,128]{3,2,1,0:T(8,128)(2,1)S(1)} %collective-permute-done.7.far_ref, bf16[64,128,128]{2,1,0:T(8,128)(2,1)S(1)} %stage.1.weights_ref), custom_call_target="tpu_custom_call" | custom-call | tf_op jit(solution)/shard_map/interpolate/pallas_call | solution.py:498
  23.0 2.6 %all-to-all-start = ((f32[32,8,128]{2,1,0:T(8,128)}), f32[32,8,128]{2,1,0:T(8,128)S(1)}, u32[]{:S(2)}, u32[]{:S(2)}) async-start(f32[32,8,128]{2,1,0:T(8,128)} %interpolate.1), calls=%async_computation | async-start | bytes 262144 | tf_op jit(solution)/shard_map/all_to_all | solution.py:510
  25.6 7.8 %all-to-all-done.own_ref = f32[32,8,128]{2,1,0:T(8,128)S(1)} async-done(((f32[32,8,128]{2,1,0:T(8,128)}), f32[32,8,128]{2,1,0:T(8,128)S(1)}, u32[]{:S(2)}, u32[]{:S(2)}) %all-to-all-start) | async-done | bytes 131104 | tf_op jit(solution)/shard_map/all_to_all | solution.py:510
  33.4 0.1 collective-permute-start.8
  33.5 0.0 collective-permute-done.6
  33.6 0.0 copy-done.2
  33.6 0.0 copy-done.3
  33.6 2.4 %flow.1 = (f32[3,8,2,4,8,128]{5,4,3,2,1,0:T(8,128)S(1)}, f32[2,8,128]{2,1,0:T(8,128)}) custom-call(f32[8]{0:T(128)S(1)} %copy-done.2, f32[8]{0:T(128)S(1)} %copy-done.3, bf16[32,4,16,128]{3,2,1,0:T(8,128)(2,1)S(1)} %bitcast.39), custom_call_target="tpu_custom_call" | custom-call | tf_op jit(solution)/shard_map/flow/pallas_call | solution.py:514
  36.0 0.0 collective-permute-done.8.other_ref
  36.0 0.0 copy-done
  36.0 0.0 copy-done.1
  36.0 1.3 %solve.1 = f32[32,8,128]{2,1,0:T(8,128)S(1)} custom-call(f32[16]{0:T(128)S(1)} %copy-done, f32[16]{0:T(128)S(1)} %copy-done.1, f32[32,8,128]{2,1,0:T(8,128)S(1)} %all-to-all-done.own_ref, f32[32,8,128]{2,1,0:T(8,128)S(1)} %collective-permute-done.8.other_ref, f32[3,8,2,4,8,128]{5,4,3,2,1,0:T(8,128)S(1)} %get-tuple-element.5.flux_ref), custom_call_target="tpu_custom_call" | custom-call | tf_op jit(solution)/shard_map/solve/pallas_call | solution.py:527
  37.3 9.8 %all_to_all.10 = f32[32,8,128]{2,1,0:T(8,128)S(1)} all-to-all(f32[32,8,128]{2,1,0:T(8,128)S(1)} %solve.1), channel_id=1, replica_groups=mesh['gx'=4,'gy'=2,'gz'=4] {'gx','gy','gz'}, dimensions={0} | all-to-all | bytes 262144 | tf_op jit(solution)/shard_map/all_to_all | solution.py:536
  47.1 0.7 %copy.15 = f32[2,8,2,8,128]{4,3,2,1,0:T(8,128)} copy(f32[2,8,2,8,128]{4,3,1,2,0:T(8,128)S(1)} %bitcast.42) | data formatting | bytes 262144 | tf_op jit(solution)/shard_map/transpose | solution.py:538
  (9 shorter events, 0.2 us)
Async XLA Ops:
  1.6 7.1 %collective-permute-start.2 = (bf16[20,16,128]{2,1,0:T(8,128)(2,1)S(1)}, bf16[20,16,128]{2,1,0:T(8,128)(2,1)S(1)}, u32[]{:S(2)}, u32[]{:S(2)}) collective-permute-start(bf16[20,16,128]{2,1,0:T(8,128)(2,1)S(1)} %pack.1), channel_id=1, source_target_pairs={{0,20},{4,16},{8,28},{12,24},{16,4},{20,0},{24,12},{28,8},{1,21},{... | collective-permute-start | bytes 245768 | tf_op jit(solution)/shard_map/ppermute | solution.py:407
  5.6 4.4 %collective-permute-start.1 = (bf16[20,16,128]{2,1,0:T(8,128)(2,1)S(1)}, bf16[20,16,128]{2,1,0:T(8,128)(2,1)S(1)}, u32[]{:S(2)}, u32[]{:S(2)}) collective-permute-start(bf16[20,16,128]{2,1,0:T(8,128)(2,1)S(1)} %pack.1), channel_id=1, source_target_pairs={{0,16},{4,20},{8,24},{12,28},{16,0},{20,4},{24,8},{28,12},{1,17},{... | collective-permute-start | bytes 245768 | tf_op jit(solution)/shard_map/ppermute | solution.py:407
  6.1 4.4 %collective-permute-start = (bf16[20,16,128]{2,1,0:T(8,128)(2,1)S(1)}, bf16[20,16,128]{2,1,0:T(8,128)(2,1)S(1)}, u32[]{:S(2)}, u32[]{:S(2)}) collective-permute-start(bf16[20,16,128]{2,1,0:T(8,128)(2,1)S(1)} %pack.1), channel_id=1, source_target_pairs={{0,4},{4,0},{8,12},{12,8},{16,20},{20,16},{24,28},{28,24},{1,5},{5... | collective-permute-start | bytes 245768 | tf_op jit(solution)/shard_map/ppermute | solution.py:407
  6.9 1.7 %copy-start.4 = (s32[1,1,1,64]{3,2,1,0:T(1,128)S(1)}, s32[1,1,1,64]{3,2,1,0:T(1,128)}, u32[]{:S(2)}) copy-start(s32[1,1,1,64]{3,2,1,0:T(1,128)} %param.22) | copy-start | bytes 772
  6.9 1.7 %copy-start.5 = (s32[1,1,1,64]{3,2,1,0:T(1,128)S(1)}, s32[1,1,1,64]{3,2,1,0:T(1,128)}, u32[]{:S(2)}) copy-start(s32[1,1,1,64]{3,2,1,0:T(1,128)} %param.24) | copy-start | bytes 772
  6.9 1.7 %copy-start.6 = (s32[1,1,1,64,1]{3,4,2,1,0:T(1,128)S(1)}, s32[1,1,1,64,1]{3,4,2,1,0:T(1,128)}, u32[]{:S(2)}) copy-start(s32[1,1,1,64,1]{3,4,2,1,0:T(1,128)} %param.23) | copy-start | bytes 772
  10.6 5.3 %collective-permute-start.4 = (bf16[4,4,16,128]{3,2,1,0:T(8,128)(2,1)S(1)}, bf16[4,4,16,128]{3,2,1,0:T(8,128)(2,1)S(1)}, u32[]{:S(2)}, u32[]{:S(2)}) collective-permute-start(bf16[4,4,16,128]{3,2,1,0:T(8,128)(2,1)S(1)} %get-tuple-element.7), channel_id=1, source_target_pairs={{0,2},{1,3},{2,0},{3,1},{4,6},{5,7},{6,4},{7,5},{8,10},{9,11},{10,... | collective-permute-start | bytes 196616 | tf_op jit(solution)/shard_map/ppermute | solution.py:423
  13.2 4.3 %collective-permute-start.3 = (bf16[4,4,16,128]{3,2,1,0:T(8,128)(2,1)S(1)}, bf16[4,4,16,128]{3,2,1,0:T(8,128)(2,1)S(1)}, u32[]{:S(2)}, u32[]{:S(2)}) collective-permute-start(bf16[4,4,16,128]{3,2,1,0:T(8,128)(2,1)S(1)} %get-tuple-element.7), channel_id=1, source_target_pairs={{0,1},{1,0},{2,3},{3,2},{4,5},{5,4},{6,7},{7,6},{8,9},{9,8},{10,11... | collective-permute-start | bytes 196616 | tf_op jit(solution)/shard_map/ppermute | solution.py:423
  14.8 6.1 %collective-permute-start.5 = (bf16[4,4,16,128]{3,2,1,0:T(8,128)(2,1)S(1)}, bf16[4,4,16,128]{3,2,1,0:T(8,128)(2,1)S(1)}, u32[]{:S(2)}, u32[]{:S(2)}) collective-permute-start(bf16[4,4,16,128]{3,2,1,0:T(8,128)(2,1)S(1)} %get-tuple-element.7), channel_id=1, source_target_pairs={{0,3},{1,2},{2,1},{3,0},{4,7},{5,6},{6,5},{7,4},{8,11},{9,10},{10,... | collective-permute-start | bytes 196616 | tf_op jit(solution)/shard_map/ppermute | solution.py:423
  15.0 6.0 %collective-permute-start.7 = (bf16[4,20,16,128]{3,2,1,0:T(8,128)(2,1)S(1)}, bf16[4,20,16,128]{3,2,1,0:T(8,128)(2,1)S(1)}, u32[]{:S(2)}, u32[]{:S(2)}) collective-permute-start(bf16[4,20,16,128]{3,2,1,0:T(8,128)(2,1)S(1)} %pad_maximum_fusion.near_ref), channel_id=1, source_target_pairs={{0,8},{4,12},{8,0},{12,4},{16,24},{20,28},{24,16},{28,20},{1,9},{5... | collective-permute-start | bytes 983048 | tf_op jit(solution)/shard_map/ppermute | solution.py:407
  20.9 12.7 %copy-start.2 = (f32[8]{0:T(128)S(1)}, f32[8]{0:T(128)}, u32[]{:S(2)}) copy-start(f32[8]{0:T(128)} %cond_ref.1) | copy-start | bytes 100
  20.9 12.7 %copy-start.3 = (f32[8]{0:T(128)S(1)}, f32[8]{0:T(128)}, u32[]{:S(2)}) copy-start(f32[8]{0:T(128)} %alpha_ref.1) | copy-start | bytes 100
  20.9 15.1 %copy-start = (f32[16]{0:T(128)S(1)}, f32[16]{0:T(128)}, u32[]{:S(2)}) copy-start(f32[16]{0:T(128)} %mol_ref.1) | copy-start | bytes 196
  21.0 15.0 %copy-start.1 = (f32[16]{0:T(128)S(1)}, f32[16]{0:T(128)}, u32[]{:S(2)}) copy-start(f32[16]{0:T(128)} %long_ref.1) | copy-start | bytes 196
  21.0 12.6 %collective-permute-start.6 = (bf16[4,4,4,16,128]{4,3,2,1,0:T(8,128)(2,1)S(1)}, bf16[4,4,4,16,128]{4,3,2,1,0:T(8,128)(2,1)S(1)}, u32[]{:S(2)}, u32[]{:S(2)}) collective-permute-start(bf16[4,4,4,16,128]{4,3,2,1,0:T(8,128)(2,1)S(1)} %pad_maximum_fusion.1), channel_id=1, source_target_pairs={{0,8},{4,12},{8,0},{12,4},{16,24},{20,28},{24,16},{28,20},{1,9},{5... | collective-permute-start | bytes 786440 | tf_op jit(solution)/shard_map/ppermute | solution.py:407
  23.0 10.4 %all-to-all-start = ((f32[32,8,128]{2,1,0:T(8,128)}), f32[32,8,128]{2,1,0:T(8,128)S(1)}, u32[]{:S(2)}, u32[]{:S(2)}) async-start(f32[32,8,128]{2,1,0:T(8,128)} %interpolate.1), calls=%async_computation | async-start | bytes 262144 | tf_op jit(solution)/shard_map/all_to_all | solution.py:510
  33.4 2.6 %collective-permute-start.8 = (f32[32,8,128]{2,1,0:T(8,128)S(1)}, f32[32,8,128]{2,1,0:T(8,128)S(1)}, u32[]{:S(2)}, u32[]{:S(2)}) collective-permute-start(f32[32,8,128]{2,1,0:T(8,128)S(1)} %all-to-all-done.own_ref), channel_id=1, source_target_pairs={{0,8},{4,12},{8,0},{12,4},{16,24},{20,28},{24,16},{28,20},{1,9},{5... | collective-permute-start | bytes 393224 | tf_op jit(solution)/shard_map/ppermute | solution.py:407
where the time goes:
time: 48 us; the launch traced here: 47.8 us
  waiting for transfers between devices  15.5 us (32%)
  starting transfers between devices  11.8 us (25%)
  blocking collectives  9.79 us (20%)
  Pallas kernels  8.18 us (17%)
  between operations  1.48 us (3%)
  local copies, waits for them, and re-layouts  0.81 us (2%)
    all_to_all x1, blocking collectives, field_plan(): back = lax.all_to_all(back, AXES, split_axis=0, concat_axis=0, tiled=True)  9.79 us
    all_to_all x1, waiting for transfers between devices, field_plan(): lax.all_to_all(fields, AXES, split_axis=0, concat_axis=0, tiled=True)  7.76 us
    ppermute x3, waiting for transfers between devices, from_depth(): parts.append(lax.ppermute(x, 'gz', [(i, i ^ shift) for i in range(count)]))  5.83 us
    ppermute x6, starting transfers between devices, moved(): return lax.ppermute(x, LAYER, pairs)  4.82 us
    ppermute x3, starting transfers between devices, from_depth(): parts.append(lax.ppermute(x, 'gz', [(i, i ^ shift) for i in range(count)]))  4.45 us
    all_to_all x1, starting transfers between devices, field_plan(): lax.all_to_all(fields, AXES, split_axis=0, concat_axis=0, tiled=True)  2.58 us
    pallas_call x1, Pallas kernels, field_plan(): pl.pallas_call(functools.partial(flow_kernel, shape), out_shape=(jax.Shap...  2.4 us
    pallas_call x1, Pallas kernels, field_plan(): pl.pallas_call(functools.partial(interpolate_kernel, shape[:3], solutes),...  1.95 us
  transfers between devices with their start and end apart: 10, of which 6 were waited for; matrix products, arithmetic and copies ran while one was open for 0% of the time, Pallas kernels for 12%

commit v1 on v0

--- a/solution.py
+++ b/solution.py
@@ -241,10 +241,14 @@
 
 
 def flow_kernel(
-    shape, cond_ref, alpha_ref, cells_ref, flux_ref, head_ref, h_s, q_s, k_s, a_s, w_s
+    shape, cond_ref, alpha_ref, mol_ref, long_ref, cells_ref, face_ref, edge_ref, head_ref, h_s, q_s, k_s, a_s, w_s
 ):
     blocks_x, blocks_y, blocks_z, cells_x = shape
     mine_x, mine_y, mine_z = (lax.axis_index(axis) for axis in AXES)
+    solute = ((mine_x // 2) * blocks_y + mine_y) * blocks_z + mine_z
+    mol = disp_time * mol_ref[solute]
+    lng = disp_time * long_ref[solute]
+    edge_ref[...] = jnp.full(edge_ref.shape, mol + lng, jnp.float32)
     planes = blocks_x * cells_x
     plane_shape = h_s.shape[1:]
     zones = cond_ref.shape[0]
@@ -295,15 +299,15 @@
             h_s[plane] = h + time_step * (net - pump_rate * w_s[plane])
             from_below = in_x
             if sweep == RSTEPS - 1:
-                flux_ref[0, plane] = jnp.sqrt(1.0 + in_x * in_x)
-                flux_ref[1, plane] = jnp.sqrt(1.0 + in_y * in_y)
-                flux_ref[2, plane] = jnp.sqrt(1.0 + in_z * in_z)
+                face_ref[0, plane] = mol + lng * jnp.sqrt(1.0 + in_x * in_x)
+                face_ref[1, plane] = mol + lng * jnp.sqrt(1.0 + in_y * in_y)
+                face_ref[2, plane] = mol + lng * jnp.sqrt(1.0 + in_z * in_z)
     for i in range(cells_x):
         head_ref[i] = h_s[mine_x * cells_x + i, mine_y, mine_z]
 
 
 def interpolate_kernel(shape, solutes, table_ref, near_ref, far_ref, weights_ref, out_ref, sum_s, all_s):
-    entries, _ = weights_ref.shape[:2]
+    entries, tile_len = weights_ref.shape[:2]
     _, blocks_y, blocks_z = shape
     rows_sent = out_ref.shape[1]
     tile_count = 2 * rows_sent
@@ -314,10 +318,21 @@
             all_s[(chips + c) * tile_count + t] = far_ref[c, t]
     for t in range(tile_count):
         sum_s[t * solutes : (t + 1) * solutes, :] = near_ref[0, t].astype(jnp.float32)
-    for e in range(entries):
-        got = jnp.dot(all_s[table_ref[e]], weights_ref[e], preferred_element_type=jnp.float32)
-        rows = pl.ds(pl.multiple_of(table_ref[entries + e] * solutes, solutes), solutes)
-        sum_s[rows, :] = sum_s[rows, :] + got
+    none = jnp.zeros((solutes, tile_len), jnp.bfloat16)
+    for e in range(0, entries, 4):
+        tiles = [all_s[table_ref[e + n]] for n in range(4)]
+        first = jnp.concatenate([tiles[0], tiles[1], none, none], axis=0)
+        second = jnp.concatenate([none, none, tiles[2], tiles[3]], axis=0)
+        sources = jnp.concatenate([first, second], axis=1)
+        above = jnp.concatenate([weights_ref[e], weights_ref[e + 1]], axis=1)
+        below = jnp.concatenate([weights_ref[e + 2], weights_ref[e + 3]], axis=1)
+        matrices = jnp.concatenate([above, below], axis=0)
+        got = jnp.dot(sources, matrices, preferred_element_type=jnp.float32)
+        for n in range(4):
+            rows = pl.ds(pl.multiple_of(table_ref[entries + e + n] * solutes, solutes), solutes)
+            column = n % 2 * tile_len
+            part = got[n * solutes : (n + 1) * solutes, column : column + tile_len]
+            sum_s[rows, :] = sum_s[rows, :] + part
     for s in range(solutes):
         field = sum_s[pl.ds(s, tile_count, stride=solutes), :]
         per = blocks_y * blocks_z
@@ -326,8 +341,8 @@
         out_ref[low + per] = field[rows_sent:]
 
 
-def spread_out(v, above, below_x, fluxes, mol, lng, edge_w):
-    w_x, w_y, w_z = [mol + lng * f for f in fluxes]
+def spread_out(v, above, below_x, faces, edge_w):
+    w_x, w_y, w_z = faces
     if above is None:
         f_x = w_x * v
     else:
@@ -344,17 +359,13 @@
     return out + (f_z - at_previous(f_z, 1, 3, low_z)), f_x
 
 
-def solve_kernel(shape, mol_ref, long_ref, own_ref, other_ref, flux_ref, out_ref, v_s, y_s):
+def solve_kernel(shape, own_ref, other_ref, face_ref, edge_ref, out_ref, v_s, y_s):
     blocks_x, blocks_y, blocks_z, cells_x = shape
     per = blocks_y * blocks_z
     planes = blocks_x * cells_x
-    plane_shape = flux_ref.shape[2:]
-    me_x, me_y, me_z = (lax.axis_index(axis) for axis in AXES)
-    solute = ((me_x // 2) * blocks_y + me_y) * blocks_z + me_z
-    part = me_x % 2
-    mol = disp_time * mol_ref[solute]
-    lng = disp_time * long_ref[solute]
-    edge_w = mol + lng
+    plane_shape = face_ref.shape[2:]
+    part = lax.axis_index(AXES[0]) % 2
+    edge_w = edge_ref[...]
     parts = jnp.full((per,) + plane_shape[2:], part, jnp.int32)
     for plane in range(planes):
         a, i = plane // cells_x, plane % cells_x
@@ -370,8 +381,8 @@
     for plane in range(planes):
         v = v_s[plane]
         above = v_s[plane + 1] if plane < planes - 1 else None
-        fluxes = [flux_ref[n, plane] for n in range(3)]
-        y, below = spread_out(v, above, below, fluxes, mol, lng, edge_w)
+        faces = [face_ref[n, plane] for n in range(3)]
+        y, below = spread_out(v, above, below, faces, edge_w)
         y_s[plane] = y
         p[0] += total(v * v)
         p[1] += total(v * y)
@@ -380,8 +391,8 @@
     for plane in range(planes):
         v = y_s[plane]
         above = y_s[plane + 1] if plane < planes - 1 else None
-        fluxes = [flux_ref[n, plane] for n in range(3)]
-        z, below = spread_out(v, above, below, fluxes, mol, lng, edge_w)
+        faces = [face_ref[n, plane] for n in range(3)]
+        z, below = spread_out(v, above, below, faces, edge_w)
         p[3] += total(v * z)
     p0, p1, p2, p3 = [jnp.sum(x, axis=(0, 1), keepdims=True) for x in p]
     d = p1 / p0
@@ -506,33 +517,34 @@
         ],
         compiler_params=grant(8),
         name="interpolate",
-    )(table, near, far, weights)
+    )(pltpu.with_memory_space_constraint(table, pltpu.SMEM), near, far, weights)
     field = lax.all_to_all(fields, AXES, split_axis=0, concat_axis=0, tiled=True)
     other = moved(field, 1, 0)
 
     grid_scratch = pltpu.VMEM((planes,) + plane_shape, f32)
-    flux, head = pl.pallas_call(
+    faces, edge, head = pl.pallas_call(
         functools.partial(flow_kernel, shape),
         out_shape=(
             jax.ShapeDtypeStruct((3, planes) + plane_shape, f32),
+            jax.ShapeDtypeStruct((cells_y, tile_len), f32),
             jax.ShapeDtypeStruct((cells_x, cells_y, tile_len), f32),
         ),
-        in_specs=[SMEM(), SMEM(), VMEM()],
-        out_specs=(VMEM(), VMEM()),
+        in_specs=[SMEM()] * 4 + [VMEM()],
+        out_specs=(VMEM(),) * 3,
         scratch_shapes=[grid_scratch] * 5,
         compiler_params=grant(8),
         name="flow",
-    )(zone_conductivity, zone_alpha, cells)
+    )(zone_conductivity, zone_alpha, disp_molecular, disp_longitudinal, cells)
 
     back = pl.pallas_call(
         functools.partial(solve_kernel, shape),
         out_shape=jax.ShapeDtypeStruct(field.shape, f32),
-        in_specs=[SMEM(), SMEM(), VMEM(), VMEM(), VMEM()],
+        in_specs=[VMEM()] * 4,
         out_specs=VMEM(),
         scratch_shapes=[grid_scratch] * 2,
         compiler_params=grant(8),
         name="solve",
-    )(disp_molecular, disp_longitudinal, field, other, flux)
+    )(field, other, faces, edge)
     back = lax.all_to_all(back, AXES, split_axis=0, concat_axis=0, tiled=True)
     back = back.reshape((blocks_x // 2, 2, blocks_y * blocks_z, cells_y, tile_len))
     back = back.transpose(0, 2, 1, 3, 4)

time: 48 us -> 47.3 us (0.985)
  Pallas kernels: 8.18 us -> 7.41 us
    pallas_call x1, Pallas kernels: 1.29 us -> 0.66 us  [field_plan(): pl.pallas_call(functools.partial(solve_kernel, shape), out_shape=jax.Shap...]
where the time goes in v1:
time: 47.3 us; the launch traced here: 47 us
  waiting for transfers between devices  15.5 us (33%)
  starting transfers between devices  11.8 us (25%)
  blocking collectives  9.79 us (21%)
  Pallas kernels  7.41 us (16%)
  between operations  1.5 us (3%)
  local copies, waits for them, and re-layouts  0.81 us (2%)
    all_to_all x1, blocking collectives, field_plan(): back = lax.all_to_all(back, AXES, split_axis=0, concat_axis=0, tiled=True)  9.79 us
    all_to_all x1, waiting for transfers between devices, field_plan(): lax.all_to_all(fields, AXES, split_axis=0, concat_axis=0, tiled=True)  7.76 us
    ppermute x3, waiting for transfers between devices, from_depth(): parts.append(lax.ppermute(x, 'gz', [(i, i ^ shift) for i in range(count)]))  5.83 us
    ppermute x6, starting transfers between devices, moved(): return lax.ppermute(x, LAYER, pairs)  4.82 us
    ppermute x3, starting transfers between devices, from_depth(): parts.append(lax.ppermute(x, 'gz', [(i, i ^ shift) for i in range(count)]))  4.45 us
    all_to_all x1, starting transfers between devices, field_plan(): lax.all_to_all(fields, AXES, split_axis=0, concat_axis=0, tiled=True)  2.58 us
    pallas_call x1, Pallas kernels, field_plan(): pl.pallas_call(functools.partial(flow_kernel, shape), out_shape=(jax.Shap...  2.42 us
    ppermute x6, waiting for transfers between devices, moved(): return lax.ppermute(x, LAYER, pairs)  1.86 us
  transfers between devices with their start and end apart: 10, of which 6 were waited for; matrix products, arithmetic and copies ran while one was open for 0% of the time, Pallas kernels for 12%

profile of v1, /device:TPU:0, one launch (start us, length us, event | category | flops | bytes accessed | tf_op | source)
XLA Modules:
  0.0 47.0 jit_solution(13630774770831186617)
XLA Ops:
  0.6 0.9 %pack.1 = bf16[20,16,128]{2,1,0:T(8,128)(2,1)S(1)} custom-call(bf16[16,16,128]{2,1,0:T(8,128)(2,1)} %bitcast.50, f32[2,8,128]{2,1,0:T(8,128)} %head_ref.1, s32[2,8,128]{2,1,0:T(8,128)} %zone_ref.1, s32[2,8,128]{2,1,0:T(8,128)} %well_ref.1), custom_call_target="tpu_custom_call" | custom-call | tf_op jit(solution)/shard_map/pack/pallas_call | solution.py:465
  1.6 4.0 %collective-permute-start.2 = (bf16[20,16,128]{2,1,0:T(8,128)(2,1)S(1)}, bf16[20,16,128]{2,1,0:T(8,128)(2,1)S(1)}, u32[]{:S(2)}, u32[]{:S(2)}) collective-permute-start(bf16[20,16,128]{2,1,0:T(8,128)(2,1)S(1)} %pack.1), channel_id=1, source_target_pairs={{0,20},{4,16},{8,28},{12,24},{16,4},{20,0},{24,12},{28,8},{1,21},{... | collective-permute-start | bytes 245768 | tf_op jit(solution)/shard_map/ppermute | solution.py:418
  5.6 0.5 %collective-permute-start.1 = (bf16[20,16,128]{2,1,0:T(8,128)(2,1)S(1)}, bf16[20,16,128]{2,1,0:T(8,128)(2,1)S(1)}, u32[]{:S(2)}, u32[]{:S(2)}) collective-permute-start(bf16[20,16,128]{2,1,0:T(8,128)(2,1)S(1)} %pack.1), channel_id=1, source_target_pairs={{0,16},{4,20},{8,24},{12,28},{16,0},{20,4},{24,8},{28,12},{1,17},{... | collective-permute-start | bytes 245768 | tf_op jit(solution)/shard_map/ppermute | solution.py:418
  6.1 0.1 collective-permute-start
  6.9 0.0 copy-start.4
  6.9 0.0 copy-start.5
  6.9 0.0 copy-start.6
  6.9 1.6 %stage.1.weights_ref = bf16[64,128,128]{2,1,0:T(8,128)(2,1)S(1)} custom-call(bf16[64,128,128]{2,1,0:T(8,128)(2,1)} %bitcast.41), custom_call_target="tpu_custom_call" | custom-call | tf_op jit(solution)/shard_map/stage/pallas_call | solution.py:489
  8.5 0.0 copy-done.4
  8.5 0.0 copy-done.5
  8.5 0.0 copy-done.6
  8.6 0.1 pad_add_fusion.table_ref
  8.7 0.0 collective-permute-done.2
  8.7 1.3 %collective-permute-done.1 = bf16[20,16,128]{2,1,0:T(8,128)(2,1)S(1)} collective-permute-done((bf16[20,16,128]{2,1,0:T(8,128)(2,1)S(1)}, bf16[20,16,128]{2,1,0:T(8,128)(2,1)S(1)}, u32[]{:S(2)}, u32[]{:S(2)}) %collective-permute-start.1) | collective-permute-done | bytes 81952 | tf_op jit(solution)/shard_map/ppermute | solution.py:418
  10.0 0.5 %collective-permute-done = bf16[20,16,128]{2,1,0:T(8,128)(2,1)S(1)} collective-permute-done((bf16[20,16,128]{2,1,0:T(8,128)(2,1)S(1)}, bf16[20,16,128]{2,1,0:T(8,128)(2,1)S(1)}, u32[]{:S(2)}, u32[]{:S(2)}) %collective-permute-start) | collective-permute-done | bytes 81952 | tf_op jit(solution)/shard_map/ppermute | solution.py:418
  10.6 2.7 %collective-permute-start.4 = (bf16[4,4,16,128]{3,2,1,0:T(8,128)(2,1)S(1)}, bf16[4,4,16,128]{3,2,1,0:T(8,128)(2,1)S(1)}, u32[]{:S(2)}, u32[]{:S(2)}) collective-permute-start(bf16[4,4,16,128]{3,2,1,0:T(8,128)(2,1)S(1)} %get-tuple-element.9), channel_id=1, source_target_pairs={{0,2},{1,3},{2,0},{3,1},{4,6},{5,7},{6,4},{7,5},{8,10},{9,11},{10,... | collective-permute-start | bytes 196616 | tf_op jit(solution)/shard_map/ppermute | solution.py:434
  13.2 1.6 %collective-permute-start.3 = (bf16[4,4,16,128]{3,2,1,0:T(8,128)(2,1)S(1)}, bf16[4,4,16,128]{3,2,1,0:T(8,128)(2,1)S(1)}, u32[]{:S(2)}, u32[]{:S(2)}) collective-permute-start(bf16[4,4,16,128]{3,2,1,0:T(8,128)(2,1)S(1)} %get-tuple-element.9), channel_id=1, source_target_pairs={{0,1},{1,0},{2,3},{3,2},{4,5},{5,4},{6,7},{7,6},{8,9},{9,8},{10,11... | collective-permute-start | bytes 196616 | tf_op jit(solution)/shard_map/ppermute | solution.py:434
  14.8 0.2 collective-permute-start.5
  15.0 0.0 collective-permute-start.7
  15.0 0.9 %collective-permute-done.4 = bf16[4,4,16,128]{3,2,1,0:T(8,128)(2,1)S(1)} collective-permute-done((bf16[4,4,16,128]{3,2,1,0:T(8,128)(2,1)S(1)}, bf16[4,4,16,128]{3,2,1,0:T(8,128)(2,1)S(1)}, u32[]{:S(2)}, u32[]{:S(2)}) %collective-permute-start.4) | collective-permute-done | bytes 65568 | tf_op jit(solution)/shard_map/ppermute | solution.py:434
  15.9 1.6 %collective-permute-done.3 = bf16[4,4,16,128]{3,2,1,0:T(8,128)(2,1)S(1)} collective-permute-done((bf16[4,4,16,128]{3,2,1,0:T(8,128)(2,1)S(1)}, bf16[4,4,16,128]{3,2,1,0:T(8,128)(2,1)S(1)}, u32[]{:S(2)}, u32[]{:S(2)}) %collective-permute-start.3) | collective-permute-done | bytes 65568 | tf_op jit(solution)/shard_map/ppermute | solution.py:434
  17.5 3.4 %collective-permute-done.5 = bf16[4,4,16,128]{3,2,1,0:T(8,128)(2,1)S(1)} collective-permute-done((bf16[4,4,16,128]{3,2,1,0:T(8,128)(2,1)S(1)}, bf16[4,4,16,128]{3,2,1,0:T(8,128)(2,1)S(1)}, u32[]{:S(2)}, u32[]{:S(2)}) %collective-permute-start.5) | collective-permute-done | bytes 65568 | tf_op jit(solution)/shard_map/ppermute | solution.py:434
  20.9 0.0 copy-start
  20.9 0.0 copy-start.1
  20.9 0.0 copy-start.2
  21.0 0.0 copy-start.3
  21.0 0.1 collective-permute-start.6
  21.0 0.0 collective-permute-done.7.far_ref
  21.1 1.8 %interpolate.1 = f32[32,8,128]{2,1,0:T(8,128)} custom-call(s32[128]{0:T(128)S(1)} %pad_add_fusion.table_ref, bf16[4,20,16,128]{3,2,1,0:T(8,128)(2,1)S(1)} %pad_maximum_fusion.near_ref, bf16[4,20,16,128]{3,2,1,0:T(8,128)(2,1)S(1)} %collective-permute-done.7.far_ref, bf16[64,128,128]{2,1,0:T(8,128)(2,1)S(1)} %stage.1.weights_ref), custom_call_target="tpu_custom_call" | custom-call | tf_op jit(solution)/shard_map/interpolate/pallas_call | solution.py:509
  22.8 2.6 %all-to-all-start = ((f32[32,8,128]{2,1,0:T(8,128)}), f32[32,8,128]{2,1,0:T(8,128)S(1)}, u32[]{:S(2)}, u32[]{:S(2)}) async-start(f32[32,8,128]{2,1,0:T(8,128)} %interpolate.1), calls=%async_computation | async-start | bytes 262144 | tf_op jit(solution)/shard_map/all_to_all | solution.py:521
  25.5 7.8 %all-to-all-done.own_ref = f32[32,8,128]{2,1,0:T(8,128)S(1)} async-done(((f32[32,8,128]{2,1,0:T(8,128)}), f32[32,8,128]{2,1,0:T(8,128)S(1)}, u32[]{:S(2)}, u32[]{:S(2)}) %all-to-all-start) | async-done | bytes 131104 | tf_op jit(solution)/shard_map/all_to_all | solution.py:521
  33.2 0.1 collective-permute-start.8
  33.3 0.0 collective-permute-done.6
  33.4 0.0 copy-done
  33.4 0.0 copy-done.1
  33.4 0.0 copy-done.2
  33.4 0.0 copy-done.3
  33.4 2.4 %flow.1 = (f32[3,8,2,4,8,128]{5,4,3,2,1,0:T(8,128)S(1)}, f32[8,128]{1,0:T(8,128)S(1)}, f32[2,8,128]{2,1,0:T(8,128)}) custom-call(f32[8]{0:T(128)S(1)} %copy-done, f32[8]{0:T(128)S(1)} %copy-done.1, f32[16]{0:T(128)S(1)} %copy-done.2, f32[16]{0:T(128)S(1)} %copy-done.3, bf16[32,4,16,128]{3,2,1,0:T(8,128)(2,1)S(1)} %bitcast.39), custom_call_target="tpu_custom_call" | custom-call | tf_op jit(solution)/shard_map/flow/pallas_call | solution.py:525
  35.9 0.0 collective-permute-done.8.other_ref
  35.9 0.7 %solve.1 = f32[32,8,128]{2,1,0:T(8,128)S(1)} custom-call(f32[32,8,128]{2,1,0:T(8,128)S(1)} %all-to-all-done.own_ref, f32[32,8,128]{2,1,0:T(8,128)S(1)} %collective-permute-done.8.other_ref, f32[3,8,2,4,8,128]{5,4,3,2,1,0:T(8,128)S(1)} %get-tuple-element.6.face_ref, f32[8,128]{1,0:T(8,128)S(1)} %get-tuple-element.7.edge_ref), custom_call_target="tpu_custom_call" | custom-call | tf_op jit(solution)/shard_map/solve/pallas_call | solution.py:539
  36.5 9.8 %all_to_all.10 = f32[32,8,128]{2,1,0:T(8,128)S(1)} all-to-all(f32[32,8,128]{2,1,0:T(8,128)S(1)} %solve.1), channel_id=1, replica_groups=mesh['gx'=4,'gy'=2,'gz'=4] {'gx','gy','gz'}, dimensions={0} | all-to-all | bytes 262144 | tf_op jit(solution)/shard_map/all_to_all | solution.py:548
  46.3 0.7 %copy.15 = f32[2,8,2,8,128]{4,3,2,1,0:T(8,128)} copy(f32[2,8,2,8,128]{4,3,1,2,0:T(8,128)S(1)} %bitcast.42) | data formatting | bytes 262144 | tf_op jit(solution)/shard_map/transpose | solution.py:550
  (9 shorter events, 0.2 us)
Async XLA Ops:
  1.6 7.1 %collective-permute-start.2 = (bf16[20,16,128]{2,1,0:T(8,128)(2,1)S(1)}, bf16[20,16,128]{2,1,0:T(8,128)(2,1)S(1)}, u32[]{:S(2)}, u32[]{:S(2)}) collective-permute-start(bf16[20,16,128]{2,1,0:T(8,128)(2,1)S(1)} %pack.1), channel_id=1, source_target_pairs={{0,20},{4,16},{8,28},{12,24},{16,4},{20,0},{24,12},{28,8},{1,21},{... | collective-permute-start | bytes 245768 | tf_op jit(solution)/shard_map/ppermute | solution.py:418
  5.6 4.4 %collective-permute-start.1 = (bf16[20,16,128]{2,1,0:T(8,128)(2,1)S(1)}, bf16[20,16,128]{2,1,0:T(8,128)(2,1)S(1)}, u32[]{:S(2)}, u32[]{:S(2)}) collective-permute-start(bf16[20,16,128]{2,1,0:T(8,128)(2,1)S(1)} %pack.1), channel_id=1, source_target_pairs={{0,16},{4,20},{8,24},{12,28},{16,0},{20,4},{24,8},{28,12},{1,17},{... | collective-permute-start | bytes 245768 | tf_op jit(solution)/shard_map/ppermute | solution.py:418
  6.1 4.4 %collective-permute-start = (bf16[20,16,128]{2,1,0:T(8,128)(2,1)S(1)}, bf16[20,16,128]{2,1,0:T(8,128)(2,1)S(1)}, u32[]{:S(2)}, u32[]{:S(2)}) collective-permute-start(bf16[20,16,128]{2,1,0:T(8,128)(2,1)S(1)} %pack.1), channel_id=1, source_target_pairs={{0,4},{4,0},{8,12},{12,8},{16,20},{20,16},{24,28},{28,24},{1,5},{5... | collective-permute-start | bytes 245768 | tf_op jit(solution)/shard_map/ppermute | solution.py:418
  6.9 1.7 %copy-start.4 = (s32[1,1,1,64]{3,2,1,0:T(1,128)S(1)}, s32[1,1,1,64]{3,2,1,0:T(1,128)}, u32[]{:S(2)}) copy-start(s32[1,1,1,64]{3,2,1,0:T(1,128)} %param.22) | copy-start | bytes 772
  6.9 1.7 %copy-start.5 = (s32[1,1,1,64]{3,2,1,0:T(1,128)S(1)}, s32[1,1,1,64]{3,2,1,0:T(1,128)}, u32[]{:S(2)}) copy-start(s32[1,1,1,64]{3,2,1,0:T(1,128)} %param.24) | copy-start | bytes 772
  6.9 1.7 %copy-start.6 = (s32[1,1,1,64,1]{3,4,2,1,0:T(1,128)S(1)}, s32[1,1,1,64,1]{3,4,2,1,0:T(1,128)}, u32[]{:S(2)}) copy-start(s32[1,1,1,64,1]{3,4,2,1,0:T(1,128)} %param.23) | copy-start | bytes 772
  10.6 5.3 %collective-permute-start.4 = (bf16[4,4,16,128]{3,2,1,0:T(8,128)(2,1)S(1)}, bf16[4,4,16,128]{3,2,1,0:T(8,128)(2,1)S(1)}, u32[]{:S(2)}, u32[]{:S(2)}) collective-permute-start(bf16[4,4,16,128]{3,2,1,0:T(8,128)(2,1)S(1)} %get-tuple-element.9), channel_id=1, source_target_pairs={{0,2},{1,3},{2,0},{3,1},{4,6},{5,7},{6,4},{7,5},{8,10},{9,11},{10,... | collective-permute-start | bytes 196616 | tf_op jit(solution)/shard_map/ppermute | solution.py:434
  13.2 4.3 %collective-permute-start.3 = (bf16[4,4,16,128]{3,2,1,0:T(8,128)(2,1)S(1)}, bf16[4,4,16,128]{3,2,1,0:T(8,128)(2,1)S(1)}, u32[]{:S(2)}, u32[]{:S(2)}) collective-permute-start(bf16[4,4,16,128]{3,2,1,0:T(8,128)(2,1)S(1)} %get-tuple-element.9), channel_id=1, source_target_pairs={{0,1},{1,0},{2,3},{3,2},{4,5},{5,4},{6,7},{7,6},{8,9},{9,8},{10,11... | collective-permute-start | bytes 196616 | tf_op jit(solution)/shard_map/ppermute | solution.py:434
  14.8 6.1 %collective-permute-start.5 = (bf16[4,4,16,128]{3,2,1,0:T(8,128)(2,1)S(1)}, bf16[4,4,16,128]{3,2,1,0:T(8,128)(2,1)S(1)}, u32[]{:S(2)}, u32[]{:S(2)}) collective-permute-start(bf16[4,4,16,128]{3,2,1,0:T(8,128)(2,1)S(1)} %get-tuple-element.9), channel_id=1, source_target_pairs={{0,3},{1,2},{2,1},{3,0},{4,7},{5,6},{6,5},{7,4},{8,11},{9,10},{10,... | collective-permute-start | bytes 196616 | tf_op jit(solution)/shard_map/ppermute | solution.py:434
  15.0 6.0 %collective-permute-start.7 = (bf16[4,20,16,128]{3,2,1,0:T(8,128)(2,1)S(1)}, bf16[4,20,16,128]{3,2,1,0:T(8,128)(2,1)S(1)}, u32[]{:S(2)}, u32[]{:S(2)}) collective-permute-start(bf16[4,20,16,128]{3,2,1,0:T(8,128)(2,1)S(1)} %pad_maximum_fusion.near_ref), channel_id=1, source_target_pairs={{0,8},{4,12},{8,0},{12,4},{16,24},{20,28},{24,16},{28,20},{1,9},{5... | collective-permute-start | bytes 983048 | tf_op jit(solution)/shard_map/ppermute | solution.py:418
  20.9 12.5 %copy-start = (f32[8]{0:T(128)S(1)}, f32[8]{0:T(128)}, u32[]{:S(2)}) copy-start(f32[8]{0:T(128)} %cond_ref.1) | copy-start | bytes 100
  20.9 12.5 %copy-start.1 = (f32[8]{0:T(128)S(1)}, f32[8]{0:T(128)}, u32[]{:S(2)}) copy-start(f32[8]{0:T(128)} %alpha_ref.1) | copy-start | bytes 100
  20.9 12.5 %copy-start.2 = (f32[16]{0:T(128)S(1)}, f32[16]{0:T(128)}, u32[]{:S(2)}) copy-start(f32[16]{0:T(128)} %mol_ref.1) | copy-start | bytes 196
  21.0 12.5 %copy-start.3 = (f32[16]{0:T(128)S(1)}, f32[16]{0:T(128)}, u32[]{:S(2)}) copy-start(f32[16]{0:T(128)} %long_ref.1) | copy-start | bytes 196
  21.0 12.4 %collective-permute-start.6 = (bf16[4,4,4,16,128]{4,3,2,1,0:T(8,128)(2,1)S(1)}, bf16[4,4,4,16,128]{4,3,2,1,0:T(8,128)(2,1)S(1)}, u32[]{:S(2)}, u32[]{:S(2)}) collective-permute-start(bf16[4,4,4,16,128]{4,3,2,1,0:T(8,128)(2,1)S(1)} %pad_maximum_fusion.1), channel_id=1, source_target_pairs={{0,8},{4,12},{8,0},{12,4},{16,24},{20,28},{24,16},{28,20},{1,9},{5... | collective-permute-start | bytes 786440 | tf_op jit(solution)/shard_map/ppermute | solution.py:418
  22.8 10.4 %all-to-all-start = ((f32[32,8,128]{2,1,0:T(8,128)}), f32[32,8,128]{2,1,0:T(8,128)S(1)}, u32[]{:S(2)}, u32[]{:S(2)}) async-start(f32[32,8,128]{2,1,0:T(8,128)} %interpolate.1), calls=%async_computation | async-start | bytes 262144 | tf_op jit(solution)/shard_map/all_to_all | solution.py:521
  33.2 2.7 %collective-permute-start.8 = (f32[32,8,128]{2,1,0:T(8,128)S(1)}, f32[32,8,128]{2,1,0:T(8,128)S(1)}, u32[]{:S(2)}, u32[]{:S(2)}) collective-permute-start(f32[32,8,128]{2,1,0:T(8,128)S(1)} %all-to-all-done.own_ref), channel_id=1, source_target_pairs={{0,8},{4,12},{8,0},{12,4},{16,24},{20,28},{24,16},{28,20},{1,9},{5... | collective-permute-start | bytes 393224 | tf_op jit(solution)/shard_map/ppermute | solution.py:418

commit v2 on v1

--- a/solution.py
+++ b/solution.py
@@ -318,9 +318,10 @@
             all_s[(chips + c) * tile_count + t] = far_ref[c, t]
     for t in range(tile_count):
         sum_s[t * solutes : (t + 1) * solutes, :] = near_ref[0, t].astype(jnp.float32)
+    table = table_ref[...]
     none = jnp.zeros((solutes, tile_len), jnp.bfloat16)
     for e in range(0, entries, 4):
-        tiles = [all_s[table_ref[e + n]] for n in range(4)]
+        tiles = [all_s[table[0, e + n]] for n in range(4)]
         first = jnp.concatenate([tiles[0], tiles[1], none, none], axis=0)
         second = jnp.concatenate([none, none, tiles[2], tiles[3]], axis=0)
         sources = jnp.concatenate([first, second], axis=1)
@@ -329,7 +330,7 @@
         matrices = jnp.concatenate([above, below], axis=0)
         got = jnp.dot(sources, matrices, preferred_element_type=jnp.float32)
         for n in range(4):
-            rows = pl.ds(pl.multiple_of(table_ref[entries + e + n] * solutes, solutes), solutes)
+            rows = pl.ds(pl.multiple_of(table[0, entries + e + n] * solutes, solutes), solutes)
             column = n % 2 * tile_len
             part = got[n * solutes : (n + 1) * solutes, column : column + tile_len]
             sum_s[rows, :] = sum_s[rows, :] + part
@@ -509,7 +510,7 @@
     fields = pl.pallas_call(
         functools.partial(interpolate_kernel, shape[:3], solutes),
         out_shape=jax.ShapeDtypeStruct((devices, cells_y, tile_len), f32),
-        in_specs=[SMEM(), VMEM(), VMEM(), VMEM()],
+        in_specs=[VMEM()] * 4,
         out_specs=VMEM(),
         scratch_shapes=[
             pltpu.VMEM(((tile_count + 1) * solutes, tile_len), f32),
@@ -517,7 +518,7 @@
         ],
         compiler_params=grant(8),
         name="interpolate",
-    )(pltpu.with_memory_space_constraint(table, pltpu.SMEM), near, far, weights)
+    )(table[None], near, far, weights)
     field = lax.all_to_all(fields, AXES, split_axis=0, concat_axis=0, tiled=True)
     other = moved(field, 1, 0)
 

time: 47.3 us -> 46.8 us (0.989)
  no operation moved by 1% of the time
where the time goes in v2:
time: 46.8 us; the launch traced here: 46.6 us
  waiting for transfers between devices  15.5 us (33%)
  starting transfers between devices  11.8 us (25%)
  blocking collectives  9.79 us (21%)
  Pallas kernels  6.99 us (15%)
  between operations  1.5 us (3%)
  local copies, waits for them, and re-layouts  0.81 us (2%)
    all_to_all x1, blocking collectives, field_plan(): back = lax.all_to_all(back, AXES, split_axis=0, concat_axis=0, tiled=True)  9.79 us
    all_to_all x1, waiting for transfers between devices, field_plan(): lax.all_to_all(fields, AXES, split_axis=0, concat_axis=0, tiled=True)  7.76 us
    ppermute x3, waiting for transfers between devices, from_depth(): parts.append(lax.ppermute(x, 'gz', [(i, i ^ shift) for i in range(count)]))  5.83 us
    ppermute x6, starting transfers between devices, moved(): return lax.ppermute(x, LAYER, pairs)  4.82 us
    ppermute x3, starting transfers between devices, from_depth(): parts.append(lax.ppermute(x, 'gz', [(i, i ^ shift) for i in range(count)]))  4.45 us
    all_to_all x1, starting transfers between devices, field_plan(): lax.all_to_all(fields, AXES, split_axis=0, concat_axis=0, tiled=True)  2.58 us
    pallas_call x1, Pallas kernels, field_plan(): pl.pallas_call(functools.partial(flow_kernel, shape), out_shape=(jax.Shap...  2.42 us
    ppermute x6, waiting for transfers between devices, moved(): return lax.ppermute(x, LAYER, pairs)  1.86 us
  transfers between devices with their start and end apart: 10, of which 6 were waited for; matrix products, arithmetic and copies ran while one was open for 0% of the time, Pallas kernels for 12%

profile of v2, /device:TPU:0, one launch (start us, length us, event | category | flops | bytes accessed | tf_op | source)
XLA Modules:
  0.0 46.6 jit_solution(15847826282384227907)
XLA Ops:
  0.6 0.9 %pack.1 = bf16[20,16,128]{2,1,0:T(8,128)(2,1)S(1)} custom-call(bf16[16,16,128]{2,1,0:T(8,128)(2,1)} %bitcast.52, f32[2,8,128]{2,1,0:T(8,128)} %head_ref.1, s32[2,8,128]{2,1,0:T(8,128)} %zone_ref.1, s32[2,8,128]{2,1,0:T(8,128)} %well_ref.1), custom_call_target="tpu_custom_call" | custom-call | tf_op jit(solution)/shard_map/pack/pallas_call | solution.py:466
  1.6 4.0 %collective-permute-start.2 = (bf16[20,16,128]{2,1,0:T(8,128)(2,1)S(1)}, bf16[20,16,128]{2,1,0:T(8,128)(2,1)S(1)}, u32[]{:S(2)}, u32[]{:S(2)}) collective-permute-start(bf16[20,16,128]{2,1,0:T(8,128)(2,1)S(1)} %pack.1), channel_id=1, source_target_pairs={{0,20},{4,16},{8,28},{12,24},{16,4},{20,0},{24,12},{28,8},{1,21},{... | collective-permute-start | bytes 245768 | tf_op jit(solution)/shard_map/ppermute | solution.py:419
  5.6 0.5 %collective-permute-start.1 = (bf16[20,16,128]{2,1,0:T(8,128)(2,1)S(1)}, bf16[20,16,128]{2,1,0:T(8,128)(2,1)S(1)}, u32[]{:S(2)}, u32[]{:S(2)}) collective-permute-start(bf16[20,16,128]{2,1,0:T(8,128)(2,1)S(1)} %pack.1), channel_id=1, source_target_pairs={{0,16},{4,20},{8,24},{12,28},{16,0},{20,4},{24,8},{28,12},{1,17},{... | collective-permute-start | bytes 245768 | tf_op jit(solution)/shard_map/ppermute | solution.py:419
  6.1 0.1 collective-permute-start
  6.9 0.0 copy-start.4
  6.9 0.0 copy-start.5
  6.9 0.0 copy-start.6
  6.9 1.6 %stage.1.weights_ref = bf16[64,128,128]{2,1,0:T(8,128)(2,1)S(1)} custom-call(bf16[64,128,128]{2,1,0:T(8,128)(2,1)} %bitcast.43), custom_call_target="tpu_custom_call" | custom-call | tf_op jit(solution)/shard_map/stage/pallas_call | solution.py:490
  8.5 0.0 copy-done.4
  8.5 0.0 copy-done.5
  8.5 0.0 copy-done.6
  8.6 0.1 add_bitcast_fusion.table_ref
  8.7 0.0 collective-permute-done.2
  8.7 1.3 %collective-permute-done.1 = bf16[20,16,128]{2,1,0:T(8,128)(2,1)S(1)} collective-permute-done((bf16[20,16,128]{2,1,0:T(8,128)(2,1)S(1)}, bf16[20,16,128]{2,1,0:T(8,128)(2,1)S(1)}, u32[]{:S(2)}, u32[]{:S(2)}) %collective-permute-start.1) | collective-permute-done | bytes 81952 | tf_op jit(solution)/shard_map/ppermute | solution.py:419
  10.0 0.5 %collective-permute-done = bf16[20,16,128]{2,1,0:T(8,128)(2,1)S(1)} collective-permute-done((bf16[20,16,128]{2,1,0:T(8,128)(2,1)S(1)}, bf16[20,16,128]{2,1,0:T(8,128)(2,1)S(1)}, u32[]{:S(2)}, u32[]{:S(2)}) %collective-permute-start) | collective-permute-done | bytes 81952 | tf_op jit(solution)/shard_map/ppermute | solution.py:419
  10.6 2.7 %collective-permute-start.4 = (bf16[4,4,16,128]{3,2,1,0:T(8,128)(2,1)S(1)}, bf16[4,4,16,128]{3,2,1,0:T(8,128)(2,1)S(1)}, u32[]{:S(2)}, u32[]{:S(2)}) collective-permute-start(bf16[4,4,16,128]{3,2,1,0:T(8,128)(2,1)S(1)} %get-tuple-element.9), channel_id=1, source_target_pairs={{0,2},{1,3},{2,0},{3,1},{4,6},{5,7},{6,4},{7,5},{8,10},{9,11},{10,... | collective-permute-start | bytes 196616 | tf_op jit(solution)/shard_map/ppermute | solution.py:435
  13.2 1.6 %collective-permute-start.3 = (bf16[4,4,16,128]{3,2,1,0:T(8,128)(2,1)S(1)}, bf16[4,4,16,128]{3,2,1,0:T(8,128)(2,1)S(1)}, u32[]{:S(2)}, u32[]{:S(2)}) collective-permute-start(bf16[4,4,16,128]{3,2,1,0:T(8,128)(2,1)S(1)} %get-tuple-element.9), channel_id=1, source_target_pairs={{0,1},{1,0},{2,3},{3,2},{4,5},{5,4},{6,7},{7,6},{8,9},{9,8},{10,11... | collective-permute-start | bytes 196616 | tf_op jit(solution)/shard_map/ppermute | solution.py:435
  14.8 0.2 collective-permute-start.5
  15.0 0.0 collective-permute-start.7
  15.0 0.9 %collective-permute-done.4 = bf16[4,4,16,128]{3,2,1,0:T(8,128)(2,1)S(1)} collective-permute-done((bf16[4,4,16,128]{3,2,1,0:T(8,128)(2,1)S(1)}, bf16[4,4,16,128]{3,2,1,0:T(8,128)(2,1)S(1)}, u32[]{:S(2)}, u32[]{:S(2)}) %collective-permute-start.4) | collective-permute-done | bytes 65568 | tf_op jit(solution)/shard_map/ppermute | solution.py:435
  15.9 1.6 %collective-permute-done.3 = bf16[4,4,16,128]{3,2,1,0:T(8,128)(2,1)S(1)} collective-permute-done((bf16[4,4,16,128]{3,2,1,0:T(8,128)(2,1)S(1)}, bf16[4,4,16,128]{3,2,1,0:T(8,128)(2,1)S(1)}, u32[]{:S(2)}, u32[]{:S(2)}) %collective-permute-start.3) | collective-permute-done | bytes 65568 | tf_op jit(solution)/shard_map/ppermute | solution.py:435
  17.5 3.4 %collective-permute-done.5 = bf16[4,4,16,128]{3,2,1,0:T(8,128)(2,1)S(1)} collective-permute-done((bf16[4,4,16,128]{3,2,1,0:T(8,128)(2,1)S(1)}, bf16[4,4,16,128]{3,2,1,0:T(8,128)(2,1)S(1)}, u32[]{:S(2)}, u32[]{:S(2)}) %collective-permute-start.5) | collective-permute-done | bytes 65568 | tf_op jit(solution)/shard_map/ppermute | solution.py:435
  20.9 0.0 copy-start
  20.9 0.0 copy-start.1
  20.9 0.0 copy-start.2
  21.0 0.0 copy-start.3
  21.0 0.1 collective-permute-start.6
  21.0 0.0 collective-permute-done.7.far_ref
  21.1 1.4 %interpolate.1 = f32[32,8,128]{2,1,0:T(8,128)} custom-call(s32[1,128]{1,0:T(1,128)S(1)} %add_bitcast_fusion.table_ref, bf16[4,20,16,128]{3,2,1,0:T(8,128)(2,1)S(1)} %pad_maximum_fusion.near_ref, bf16[4,20,16,128]{3,2,1,0:T(8,128)(2,1)S(1)} %collective-permute-done.7.far_ref, bf16[64,128,128]{2,1,0:T(8,128)(2,1)S(1)} %stage.1.weights_ref), custom_call_target="tpu_custom_call" | custom-call | tf_op jit(solution)/shard_map/interpolate/pallas_call | solution.py:510
  22.4 2.6 %all-to-all-start = ((f32[32,8,128]{2,1,0:T(8,128)}), f32[32,8,128]{2,1,0:T(8,128)S(1)}, u32[]{:S(2)}, u32[]{:S(2)}) async-start(f32[32,8,128]{2,1,0:T(8,128)} %interpolate.1), calls=%async_computation | async-start | bytes 262144 | tf_op jit(solution)/shard_map/all_to_all | solution.py:522
  25.0 7.8 %all-to-all-done.own_ref = f32[32,8,128]{2,1,0:T(8,128)S(1)} async-done(((f32[32,8,128]{2,1,0:T(8,128)}), f32[32,8,128]{2,1,0:T(8,128)S(1)}, u32[]{:S(2)}, u32[]{:S(2)}) %all-to-all-start) | async-done | bytes 131104 | tf_op jit(solution)/shard_map/all_to_all | solution.py:522
  32.8 0.1 collective-permute-start.8
  32.9 0.0 collective-permute-done.6
  33.0 0.0 copy-done
  33.0 0.0 copy-done.1
  33.0 0.0 copy-done.2
  33.0 0.0 copy-done.3
  33.0 2.4 %flow.1 = (f32[3,8,2,4,8,128]{5,4,3,2,1,0:T(8,128)S(1)}, f32[8,128]{1,0:T(8,128)S(1)}, f32[2,8,128]{2,1,0:T(8,128)}) custom-call(f32[8]{0:T(128)S(1)} %copy-done, f32[8]{0:T(128)S(1)} %copy-done.1, f32[16]{0:T(128)S(1)} %copy-done.2, f32[16]{0:T(128)S(1)} %copy-done.3, bf16[32,4,16,128]{3,2,1,0:T(8,128)(2,1)S(1)} %bitcast.41), custom_call_target="tpu_custom_call" | custom-call | tf_op jit(solution)/shard_map/flow/pallas_call | solution.py:526
  35.4 0.0 collective-permute-done.8.other_ref
  35.4 0.7 %solve.1 = f32[32,8,128]{2,1,0:T(8,128)S(1)} custom-call(f32[32,8,128]{2,1,0:T(8,128)S(1)} %all-to-all-done.own_ref, f32[32,8,128]{2,1,0:T(8,128)S(1)} %collective-permute-done.8.other_ref, f32[3,8,2,4,8,128]{5,4,3,2,1,0:T(8,128)S(1)} %get-tuple-element.6.face_ref, f32[8,128]{1,0:T(8,128)S(1)} %get-tuple-element.7.edge_ref), custom_call_target="tpu_custom_call" | custom-call | tf_op jit(solution)/shard_map/solve/pallas_call | solution.py:540
  36.1 9.8 %all_to_all.10 = f32[32,8,128]{2,1,0:T(8,128)S(1)} all-to-all(f32[32,8,128]{2,1,0:T(8,128)S(1)} %solve.1), channel_id=1, replica_groups=mesh['gx'=4,'gy'=2,'gz'=4] {'gx','gy','gz'}, dimensions={0} | all-to-all | bytes 262144 | tf_op jit(solution)/shard_map/all_to_all | solution.py:549
  45.9 0.7 %copy.15 = f32[2,8,2,8,128]{4,3,2,1,0:T(8,128)} copy(f32[2,8,2,8,128]{4,3,1,2,0:T(8,128)S(1)} %bitcast.44) | data formatting | bytes 262144 | tf_op jit(solution)/shard_map/transpose | solution.py:551
  (9 shorter events, 0.2 us)
Async XLA Ops:
  1.6 7.1 %collective-permute-start.2 = (bf16[20,16,128]{2,1,0:T(8,128)(2,1)S(1)}, bf16[20,16,128]{2,1,0:T(8,128)(2,1)S(1)}, u32[]{:S(2)}, u32[]{:S(2)}) collective-permute-start(bf16[20,16,128]{2,1,0:T(8,128)(2,1)S(1)} %pack.1), channel_id=1, source_target_pairs={{0,20},{4,16},{8,28},{12,24},{16,4},{20,0},{24,12},{28,8},{1,21},{... | collective-permute-start | bytes 245768 | tf_op jit(solution)/shard_map/ppermute | solution.py:419
  5.6 4.4 %collective-permute-start.1 = (bf16[20,16,128]{2,1,0:T(8,128)(2,1)S(1)}, bf16[20,16,128]{2,1,0:T(8,128)(2,1)S(1)}, u32[]{:S(2)}, u32[]{:S(2)}) collective-permute-start(bf16[20,16,128]{2,1,0:T(8,128)(2,1)S(1)} %pack.1), channel_id=1, source_target_pairs={{0,16},{4,20},{8,24},{12,28},{16,0},{20,4},{24,8},{28,12},{1,17},{... | collective-permute-start | bytes 245768 | tf_op jit(solution)/shard_map/ppermute | solution.py:419
  6.1 4.4 %collective-permute-start = (bf16[20,16,128]{2,1,0:T(8,128)(2,1)S(1)}, bf16[20,16,128]{2,1,0:T(8,128)(2,1)S(1)}, u32[]{:S(2)}, u32[]{:S(2)}) collective-permute-start(bf16[20,16,128]{2,1,0:T(8,128)(2,1)S(1)} %pack.1), channel_id=1, source_target_pairs={{0,4},{4,0},{8,12},{12,8},{16,20},{20,16},{24,28},{28,24},{1,5},{5... | collective-permute-start | bytes 245768 | tf_op jit(solution)/shard_map/ppermute | solution.py:419
  6.9 1.7 %copy-start.4 = (s32[1,1,1,64]{3,2,1,0:T(1,128)S(1)}, s32[1,1,1,64]{3,2,1,0:T(1,128)}, u32[]{:S(2)}) copy-start(s32[1,1,1,64]{3,2,1,0:T(1,128)} %param.22) | copy-start | bytes 772
  6.9 1.7 %copy-start.5 = (s32[1,1,1,64]{3,2,1,0:T(1,128)S(1)}, s32[1,1,1,64]{3,2,1,0:T(1,128)}, u32[]{:S(2)}) copy-start(s32[1,1,1,64]{3,2,1,0:T(1,128)} %param.24) | copy-start | bytes 772
  6.9 1.7 %copy-start.6 = (s32[1,1,1,64,1]{3,4,2,1,0:T(1,128)S(1)}, s32[1,1,1,64,1]{3,4,2,1,0:T(1,128)}, u32[]{:S(2)}) copy-start(s32[1,1,1,64,1]{3,4,2,1,0:T(1,128)} %param.23) | copy-start | bytes 772
  10.6 5.3 %collective-permute-start.4 = (bf16[4,4,16,128]{3,2,1,0:T(8,128)(2,1)S(1)}, bf16[4,4,16,128]{3,2,1,0:T(8,128)(2,1)S(1)}, u32[]{:S(2)}, u32[]{:S(2)}) collective-permute-start(bf16[4,4,16,128]{3,2,1,0:T(8,128)(2,1)S(1)} %get-tuple-element.9), channel_id=1, source_target_pairs={{0,2},{1,3},{2,0},{3,1},{4,6},{5,7},{6,4},{7,5},{8,10},{9,11},{10,... | collective-permute-start | bytes 196616 | tf_op jit(solution)/shard_map/ppermute | solution.py:435
  13.2 4.3 %collective-permute-start.3 = (bf16[4,4,16,128]{3,2,1,0:T(8,128)(2,1)S(1)}, bf16[4,4,16,128]{3,2,1,0:T(8,128)(2,1)S(1)}, u32[]{:S(2)}, u32[]{:S(2)}) collective-permute-start(bf16[4,4,16,128]{3,2,1,0:T(8,128)(2,1)S(1)} %get-tuple-element.9), channel_id=1, source_target_pairs={{0,1},{1,0},{2,3},{3,2},{4,5},{5,4},{6,7},{7,6},{8,9},{9,8},{10,11... | collective-permute-start | bytes 196616 | tf_op jit(solution)/shard_map/ppermute | solution.py:435
  14.8 6.1 %collective-permute-start.5 = (bf16[4,4,16,128]{3,2,1,0:T(8,128)(2,1)S(1)}, bf16[4,4,16,128]{3,2,1,0:T(8,128)(2,1)S(1)}, u32[]{:S(2)}, u32[]{:S(2)}) collective-permute-start(bf16[4,4,16,128]{3,2,1,0:T(8,128)(2,1)S(1)} %get-tuple-element.9), channel_id=1, source_target_pairs={{0,3},{1,2},{2,1},{3,0},{4,7},{5,6},{6,5},{7,4},{8,11},{9,10},{10,... | collective-permute-start | bytes 196616 | tf_op jit(solution)/shard_map/ppermute | solution.py:435
  15.0 6.0 %collective-permute-start.7 = (bf16[4,20,16,128]{3,2,1,0:T(8,128)(2,1)S(1)}, bf16[4,20,16,128]{3,2,1,0:T(8,128)(2,1)S(1)}, u32[]{:S(2)}, u32[]{:S(2)}) collective-permute-start(bf16[4,20,16,128]{3,2,1,0:T(8,128)(2,1)S(1)} %pad_maximum_fusion.near_ref), channel_id=1, source_target_pairs={{0,8},{4,12},{8,0},{12,4},{16,24},{20,28},{24,16},{28,20},{1,9},{5... | collective-permute-start | bytes 983048 | tf_op jit(solution)/shard_map/ppermute | solution.py:419
  20.9 12.1 %copy-start = (f32[8]{0:T(128)S(1)}, f32[8]{0:T(128)}, u32[]{:S(2)}) copy-start(f32[8]{0:T(128)} %cond_ref.1) | copy-start | bytes 100
  20.9 12.1 %copy-start.1 = (f32[8]{0:T(128)S(1)}, f32[8]{0:T(128)}, u32[]{:S(2)}) copy-start(f32[8]{0:T(128)} %alpha_ref.1) | copy-start | bytes 100
  20.9 12.1 %copy-start.2 = (f32[16]{0:T(128)S(1)}, f32[16]{0:T(128)}, u32[]{:S(2)}) copy-start(f32[16]{0:T(128)} %mol_ref.1) | copy-start | bytes 196
  21.0 12.1 %copy-start.3 = (f32[16]{0:T(128)S(1)}, f32[16]{0:T(128)}, u32[]{:S(2)}) copy-start(f32[16]{0:T(128)} %long_ref.1) | copy-start | bytes 196
  21.0 12.0 %collective-permute-start.6 = (bf16[4,4,4,16,128]{4,3,2,1,0:T(8,128)(2,1)S(1)}, bf16[4,4,4,16,128]{4,3,2,1,0:T(8,128)(2,1)S(1)}, u32[]{:S(2)}, u32[]{:S(2)}) collective-permute-start(bf16[4,4,4,16,128]{4,3,2,1,0:T(8,128)(2,1)S(1)} %pad_maximum_fusion.1), channel_id=1, source_target_pairs={{0,8},{4,12},{8,0},{12,4},{16,24},{20,28},{24,16},{28,20},{1,9},{5... | collective-permute-start | bytes 786440 | tf_op jit(solution)/shard_map/ppermute | solution.py:419
  22.4 10.4 %all-to-all-start = ((f32[32,8,128]{2,1,0:T(8,128)}), f32[32,8,128]{2,1,0:T(8,128)S(1)}, u32[]{:S(2)}, u32[]{:S(2)}) async-start(f32[32,8,128]{2,1,0:T(8,128)} %interpolate.1), calls=%async_computation | async-start | bytes 262144 | tf_op jit(solution)/shard_map/all_to_all | solution.py:522
  32.8 2.7 %collective-permute-start.8 = (f32[32,8,128]{2,1,0:T(8,128)S(1)}, f32[32,8,128]{2,1,0:T(8,128)S(1)}, u32[]{:S(2)}, u32[]{:S(2)}) collective-permute-start(f32[32,8,128]{2,1,0:T(8,128)S(1)} %all-to-all-done.own_ref), channel_id=1, source_target_pairs={{0,8},{4,12},{8,0},{12,4},{16,24},{20,28},{24,16},{28,20},{1,9},{5... | collective-permute-start | bytes 393224 | tf_op jit(solution)/shard_map/ppermute | solution.py:419

commit v3 on v2

--- a/solution.py
+++ b/solution.py
@@ -215,10 +215,7 @@
 PLANES_OF_CELLS = HEAD_PARTS + 2
 
 
-def pack_kernel(conc_ref, head_ref, zone_ref, well_ref, out_ref, *scratch):
-    *held, rows_s, sems = scratch
-    fetch([conc_ref, head_ref, zone_ref, well_ref], held, sems)
-    conc_s, head_s, zone_s, well_s = held
+def pack_kernel(conc_s, head_s, zone_s, well_s, out_ref, rows_s):
     solutes, tile_count, tile_len = conc_s.shape
     for s in range(solutes):
         rows_s[s * tile_count : (s + 1) * tile_count, :] = conc_s[s].astype(jnp.float32)
@@ -462,22 +459,14 @@
     f32 = jnp.float32
 
     tiles = concentration.reshape(solutes, tile_count, tile_len)
-    block = (cells_x, cells_y, tile_len)
     packed = pl.pallas_call(
         pack_kernel,
         out_shape=jax.ShapeDtypeStruct(
             (tile_count + PLANES_OF_CELLS, solutes, tile_len), jnp.bfloat16
         ),
-        in_specs=[HBM()] * 4,
+        in_specs=[VMEM()] * 4,
         out_specs=VMEM(),
-        scratch_shapes=[
-            pltpu.VMEM(tiles.shape, jnp.bfloat16),
-            pltpu.VMEM(block, f32),
-            pltpu.VMEM(block, jnp.int32),
-            pltpu.VMEM(block, jnp.int32),
-            pltpu.VMEM((solutes * tile_count, tile_len), f32),
-            pltpu.SemaphoreType.DMA((4,)),
-        ],
+        scratch_shapes=[pltpu.VMEM((solutes * tile_count, tile_len), f32)],
         compiler_params=grant(4),
         name="pack",
     )(in_hbm(tiles), in_hbm(pressure_head), in_hbm(zone_ids), in_hbm(well_cells))

time: 46.8 us -> 46.8 us (level)
  no operation moved by 1% of the time
where the time goes in v3:
time: 46.8 us; the launch traced here: 46.6 us
  waiting for transfers between devices  15.5 us (33%)
  starting transfers between devices  11.8 us (25%)
  blocking collectives  9.79 us (21%)
  Pallas kernels  6.97 us (15%)
  between operations  1.49 us (3%)
  local copies, waits for them, and re-layouts  0.81 us (2%)
    all_to_all x1, blocking collectives, field_plan(): back = lax.all_to_all(back, AXES, split_axis=0, concat_axis=0, tiled=True)  9.79 us
    all_to_all x1, waiting for transfers between devices, field_plan(): lax.all_to_all(fields, AXES, split_axis=0, concat_axis=0, tiled=True)  7.76 us
    ppermute x3, waiting for transfers between devices, from_depth(): parts.append(lax.ppermute(x, 'gz', [(i, i ^ shift) for i in range(count)]))  5.83 us
    ppermute x6, starting transfers between devices, moved(): return lax.ppermute(x, LAYER, pairs)  4.82 us
    ppermute x3, starting transfers between devices, from_depth(): parts.append(lax.ppermute(x, 'gz', [(i, i ^ shift) for i in range(count)]))  4.45 us
    all_to_all x1, starting transfers between devices, field_plan(): lax.all_to_all(fields, AXES, split_axis=0, concat_axis=0, tiled=True)  2.58 us
    pallas_call x1, Pallas kernels, field_plan(): pl.pallas_call(functools.partial(flow_kernel, shape), out_shape=(jax.Shap...  2.42 us
    ppermute x6, waiting for transfers between devices, moved(): return lax.ppermute(x, LAYER, pairs)  1.86 us
  transfers between devices with their start and end apart: 10, of which 6 were waited for; matrix products, arithmetic and copies ran while one was open for 0% of the time, Pallas kernels for 12%

profile of v3, /device:TPU:0, one launch (start us, length us, event | category | flops | bytes accessed | tf_op | source)
XLA Modules:
  0.0 46.6 jit_solution(6068166547832994070)
XLA Ops:
  0.6 0.9 %pack.1 = bf16[20,16,128]{2,1,0:T(8,128)(2,1)S(1)} custom-call(bf16[16,16,128]{2,1,0:T(8,128)(2,1)} %bitcast.52, f32[2,8,128]{2,1,0:T(8,128)} %head_s.1, s32[2,8,128]{2,1,0:T(8,128)} %zone_s.1, s32[2,8,128]{2,1,0:T(8,128)} %well_s.1), custom_call_target="tpu_custom_call" | custom-call | tf_op jit(solution)/shard_map/pack/pallas_call | solution.py:462
  1.5 4.0 %collective-permute-start.2 = (bf16[20,16,128]{2,1,0:T(8,128)(2,1)S(1)}, bf16[20,16,128]{2,1,0:T(8,128)(2,1)S(1)}, u32[]{:S(2)}, u32[]{:S(2)}) collective-permute-start(bf16[20,16,128]{2,1,0:T(8,128)(2,1)S(1)} %pack.1), channel_id=1, source_target_pairs={{0,20},{4,16},{8,28},{12,24},{16,4},{20,0},{24,12},{28,8},{1,21},{... | collective-permute-start | bytes 245768 | tf_op jit(solution)/shard_map/ppermute | solution.py:416
  5.5 0.5 %collective-permute-start.1 = (bf16[20,16,128]{2,1,0:T(8,128)(2,1)S(1)}, bf16[20,16,128]{2,1,0:T(8,128)(2,1)S(1)}, u32[]{:S(2)}, u32[]{:S(2)}) collective-permute-start(bf16[20,16,128]{2,1,0:T(8,128)(2,1)S(1)} %pack.1), channel_id=1, source_target_pairs={{0,16},{4,20},{8,24},{12,28},{16,0},{20,4},{24,8},{28,12},{1,17},{... | collective-permute-start | bytes 245768 | tf_op jit(solution)/shard_map/ppermute | solution.py:416
  6.0 0.1 collective-permute-start
  6.8 0.0 copy-start.4
  6.8 0.0 copy-start.5
  6.9 0.0 copy-start.6
  6.9 1.6 %stage.1.weights_ref = bf16[64,128,128]{2,1,0:T(8,128)(2,1)S(1)} custom-call(bf16[64,128,128]{2,1,0:T(8,128)(2,1)} %bitcast.43), custom_call_target="tpu_custom_call" | custom-call | tf_op jit(solution)/shard_map/stage/pallas_call | solution.py:479
  8.5 0.0 copy-done.4
  8.5 0.0 copy-done.5
  8.5 0.0 copy-done.6
  8.6 0.1 add_bitcast_fusion.table_ref
  8.6 0.0 collective-permute-done.2
  8.6 1.3 %collective-permute-done.1 = bf16[20,16,128]{2,1,0:T(8,128)(2,1)S(1)} collective-permute-done((bf16[20,16,128]{2,1,0:T(8,128)(2,1)S(1)}, bf16[20,16,128]{2,1,0:T(8,128)(2,1)S(1)}, u32[]{:S(2)}, u32[]{:S(2)}) %collective-permute-start.1) | collective-permute-done | bytes 81952 | tf_op jit(solution)/shard_map/ppermute | solution.py:416
  10.0 0.5 %collective-permute-done = bf16[20,16,128]{2,1,0:T(8,128)(2,1)S(1)} collective-permute-done((bf16[20,16,128]{2,1,0:T(8,128)(2,1)S(1)}, bf16[20,16,128]{2,1,0:T(8,128)(2,1)S(1)}, u32[]{:S(2)}, u32[]{:S(2)}) %collective-permute-start) | collective-permute-done | bytes 81952 | tf_op jit(solution)/shard_map/ppermute | solution.py:416
  10.6 2.7 %collective-permute-start.4 = (bf16[4,4,16,128]{3,2,1,0:T(8,128)(2,1)S(1)}, bf16[4,4,16,128]{3,2,1,0:T(8,128)(2,1)S(1)}, u32[]{:S(2)}, u32[]{:S(2)}) collective-permute-start(bf16[4,4,16,128]{3,2,1,0:T(8,128)(2,1)S(1)} %get-tuple-element.9), channel_id=1, source_target_pairs={{0,2},{1,3},{2,0},{3,1},{4,6},{5,7},{6,4},{7,5},{8,10},{9,11},{10,... | collective-permute-start | bytes 196616 | tf_op jit(solution)/shard_map/ppermute | solution.py:432
  13.2 1.6 %collective-permute-start.3 = (bf16[4,4,16,128]{3,2,1,0:T(8,128)(2,1)S(1)}, bf16[4,4,16,128]{3,2,1,0:T(8,128)(2,1)S(1)}, u32[]{:S(2)}, u32[]{:S(2)}) collective-permute-start(bf16[4,4,16,128]{3,2,1,0:T(8,128)(2,1)S(1)} %get-tuple-element.9), channel_id=1, source_target_pairs={{0,1},{1,0},{2,3},{3,2},{4,5},{5,4},{6,7},{7,6},{8,9},{9,8},{10,11... | collective-permute-start | bytes 196616 | tf_op jit(solution)/shard_map/ppermute | solution.py:432
  14.8 0.2 collective-permute-start.5
  15.0 0.0 collective-permute-start.7
  15.0 0.9 %collective-permute-done.4 = bf16[4,4,16,128]{3,2,1,0:T(8,128)(2,1)S(1)} collective-permute-done((bf16[4,4,16,128]{3,2,1,0:T(8,128)(2,1)S(1)}, bf16[4,4,16,128]{3,2,1,0:T(8,128)(2,1)S(1)}, u32[]{:S(2)}, u32[]{:S(2)}) %collective-permute-start.4) | collective-permute-done | bytes 65568 | tf_op jit(solution)/shard_map/ppermute | solution.py:432
  15.9 1.6 %collective-permute-done.3 = bf16[4,4,16,128]{3,2,1,0:T(8,128)(2,1)S(1)} collective-permute-done((bf16[4,4,16,128]{3,2,1,0:T(8,128)(2,1)S(1)}, bf16[4,4,16,128]{3,2,1,0:T(8,128)(2,1)S(1)}, u32[]{:S(2)}, u32[]{:S(2)}) %collective-permute-start.3) | collective-permute-done | bytes 65568 | tf_op jit(solution)/shard_map/ppermute | solution.py:432
  17.5 3.4 %collective-permute-done.5 = bf16[4,4,16,128]{3,2,1,0:T(8,128)(2,1)S(1)} collective-permute-done((bf16[4,4,16,128]{3,2,1,0:T(8,128)(2,1)S(1)}, bf16[4,4,16,128]{3,2,1,0:T(8,128)(2,1)S(1)}, u32[]{:S(2)}, u32[]{:S(2)}) %collective-permute-start.5) | collective-permute-done | bytes 65568 | tf_op jit(solution)/shard_map/ppermute | solution.py:432
  20.9 0.0 copy-start
  20.9 0.0 copy-start.1
  20.9 0.0 copy-start.2
  20.9 0.0 copy-start.3
  20.9 0.1 collective-permute-start.6
  21.0 0.0 collective-permute-done.7.far_ref
  21.0 1.4 %interpolate.1 = f32[32,8,128]{2,1,0:T(8,128)} custom-call(s32[1,128]{1,0:T(1,128)S(1)} %add_bitcast_fusion.table_ref, bf16[4,20,16,128]{3,2,1,0:T(8,128)(2,1)S(1)} %pad_maximum_fusion.near_ref, bf16[4,20,16,128]{3,2,1,0:T(8,128)(2,1)S(1)} %collective-permute-done.7.far_ref, bf16[64,128,128]{2,1,0:T(8,128)(2,1)S(1)} %stage.1.weights_ref), custom_call_target="tpu_custom_call" | custom-call | tf_op jit(solution)/shard_map/interpolate/pallas_call | solution.py:499
  22.4 2.6 %all-to-all-start = ((f32[32,8,128]{2,1,0:T(8,128)}), f32[32,8,128]{2,1,0:T(8,128)S(1)}, u32[]{:S(2)}, u32[]{:S(2)}) async-start(f32[32,8,128]{2,1,0:T(8,128)} %interpolate.1), calls=%async_computation | async-start | bytes 262144 | tf_op jit(solution)/shard_map/all_to_all | solution.py:511
  25.0 7.8 %all-to-all-done.own_ref = f32[32,8,128]{2,1,0:T(8,128)S(1)} async-done(((f32[32,8,128]{2,1,0:T(8,128)}), f32[32,8,128]{2,1,0:T(8,128)S(1)}, u32[]{:S(2)}, u32[]{:S(2)}) %all-to-all-start) | async-done | bytes 131104 | tf_op jit(solution)/shard_map/all_to_all | solution.py:511
  32.8 0.1 collective-permute-start.8
  32.9 0.0 collective-permute-done.6
  33.0 0.0 copy-done
  33.0 0.0 copy-done.1
  33.0 0.0 copy-done.2
  33.0 0.0 copy-done.3
  33.0 2.4 %flow.1 = (f32[3,8,2,4,8,128]{5,4,3,2,1,0:T(8,128)S(1)}, f32[8,128]{1,0:T(8,128)S(1)}, f32[2,8,128]{2,1,0:T(8,128)}) custom-call(f32[8]{0:T(128)S(1)} %copy-done, f32[8]{0:T(128)S(1)} %copy-done.1, f32[16]{0:T(128)S(1)} %copy-done.2, f32[16]{0:T(128)S(1)} %copy-done.3, bf16[32,4,16,128]{3,2,1,0:T(8,128)(2,1)S(1)} %bitcast.41), custom_call_target="tpu_custom_call" | custom-call | tf_op jit(solution)/shard_map/flow/pallas_call | solution.py:515
  35.4 0.0 collective-permute-done.8.other_ref
  35.4 0.7 %solve.1 = f32[32,8,128]{2,1,0:T(8,128)S(1)} custom-call(f32[32,8,128]{2,1,0:T(8,128)S(1)} %all-to-all-done.own_ref, f32[32,8,128]{2,1,0:T(8,128)S(1)} %collective-permute-done.8.other_ref, f32[3,8,2,4,8,128]{5,4,3,2,1,0:T(8,128)S(1)} %get-tuple-element.6.face_ref, f32[8,128]{1,0:T(8,128)S(1)} %get-tuple-element.7.edge_ref), custom_call_target="tpu_custom_call" | custom-call | tf_op jit(solution)/shard_map/solve/pallas_call | solution.py:529
  36.1 9.8 %all_to_all.10 = f32[32,8,128]{2,1,0:T(8,128)S(1)} all-to-all(f32[32,8,128]{2,1,0:T(8,128)S(1)} %solve.1), channel_id=1, replica_groups=mesh['gx'=4,'gy'=2,'gz'=4] {'gx','gy','gz'}, dimensions={0} | all-to-all | bytes 262144 | tf_op jit(solution)/shard_map/all_to_all | solution.py:538
  45.9 0.7 %copy.15 = f32[2,8,2,8,128]{4,3,2,1,0:T(8,128)} copy(f32[2,8,2,8,128]{4,3,1,2,0:T(8,128)S(1)} %bitcast.44) | data formatting | bytes 262144 | tf_op jit(solution)/shard_map/transpose | solution.py:540
  (9 shorter events, 0.2 us)
Async XLA Ops:
  1.5 7.1 %collective-permute-start.2 = (bf16[20,16,128]{2,1,0:T(8,128)(2,1)S(1)}, bf16[20,16,128]{2,1,0:T(8,128)(2,1)S(1)}, u32[]{:S(2)}, u32[]{:S(2)}) collective-permute-start(bf16[20,16,128]{2,1,0:T(8,128)(2,1)S(1)} %pack.1), channel_id=1, source_target_pairs={{0,20},{4,16},{8,28},{12,24},{16,4},{20,0},{24,12},{28,8},{1,21},{... | collective-permute-start | bytes 245768 | tf_op jit(solution)/shard_map/ppermute | solution.py:416
  5.5 4.4 %collective-permute-start.1 = (bf16[20,16,128]{2,1,0:T(8,128)(2,1)S(1)}, bf16[20,16,128]{2,1,0:T(8,128)(2,1)S(1)}, u32[]{:S(2)}, u32[]{:S(2)}) collective-permute-start(bf16[20,16,128]{2,1,0:T(8,128)(2,1)S(1)} %pack.1), channel_id=1, source_target_pairs={{0,16},{4,20},{8,24},{12,28},{16,0},{20,4},{24,8},{28,12},{1,17},{... | collective-permute-start | bytes 245768 | tf_op jit(solution)/shard_map/ppermute | solution.py:416
  6.0 4.4 %collective-permute-start = (bf16[20,16,128]{2,1,0:T(8,128)(2,1)S(1)}, bf16[20,16,128]{2,1,0:T(8,128)(2,1)S(1)}, u32[]{:S(2)}, u32[]{:S(2)}) collective-permute-start(bf16[20,16,128]{2,1,0:T(8,128)(2,1)S(1)} %pack.1), channel_id=1, source_target_pairs={{0,4},{4,0},{8,12},{12,8},{16,20},{20,16},{24,28},{28,24},{1,5},{5... | collective-permute-start | bytes 245768 | tf_op jit(solution)/shard_map/ppermute | solution.py:416
  6.8 1.7 %copy-start.4 = (s32[1,1,1,64]{3,2,1,0:T(1,128)S(1)}, s32[1,1,1,64]{3,2,1,0:T(1,128)}, u32[]{:S(2)}) copy-start(s32[1,1,1,64]{3,2,1,0:T(1,128)} %param.22) | copy-start | bytes 772
  6.8 1.7 %copy-start.5 = (s32[1,1,1,64]{3,2,1,0:T(1,128)S(1)}, s32[1,1,1,64]{3,2,1,0:T(1,128)}, u32[]{:S(2)}) copy-start(s32[1,1,1,64]{3,2,1,0:T(1,128)} %param.24) | copy-start | bytes 772
  6.9 1.7 %copy-start.6 = (s32[1,1,1,64,1]{3,4,2,1,0:T(1,128)S(1)}, s32[1,1,1,64,1]{3,4,2,1,0:T(1,128)}, u32[]{:S(2)}) copy-start(s32[1,1,1,64,1]{3,4,2,1,0:T(1,128)} %param.23) | copy-start | bytes 772
  10.6 5.3 %collective-permute-start.4 = (bf16[4,4,16,128]{3,2,1,0:T(8,128)(2,1)S(1)}, bf16[4,4,16,128]{3,2,1,0:T(8,128)(2,1)S(1)}, u32[]{:S(2)}, u32[]{:S(2)}) collective-permute-start(bf16[4,4,16,128]{3,2,1,0:T(8,128)(2,1)S(1)} %get-tuple-element.9), channel_id=1, source_target_pairs={{0,2},{1,3},{2,0},{3,1},{4,6},{5,7},{6,4},{7,5},{8,10},{9,11},{10,... | collective-permute-start | bytes 196616 | tf_op jit(solution)/shard_map/ppermute | solution.py:432
  13.2 4.3 %collective-permute-start.3 = (bf16[4,4,16,128]{3,2,1,0:T(8,128)(2,1)S(1)}, bf16[4,4,16,128]{3,2,1,0:T(8,128)(2,1)S(1)}, u32[]{:S(2)}, u32[]{:S(2)}) collective-permute-start(bf16[4,4,16,128]{3,2,1,0:T(8,128)(2,1)S(1)} %get-tuple-element.9), channel_id=1, source_target_pairs={{0,1},{1,0},{2,3},{3,2},{4,5},{5,4},{6,7},{7,6},{8,9},{9,8},{10,11... | collective-permute-start | bytes 196616 | tf_op jit(solution)/shard_map/ppermute | solution.py:432
  14.8 6.1 %collective-permute-start.5 = (bf16[4,4,16,128]{3,2,1,0:T(8,128)(2,1)S(1)}, bf16[4,4,16,128]{3,2,1,0:T(8,128)(2,1)S(1)}, u32[]{:S(2)}, u32[]{:S(2)}) collective-permute-start(bf16[4,4,16,128]{3,2,1,0:T(8,128)(2,1)S(1)} %get-tuple-element.9), channel_id=1, source_target_pairs={{0,3},{1,2},{2,1},{3,0},{4,7},{5,6},{6,5},{7,4},{8,11},{9,10},{10,... | collective-permute-start | bytes 196616 | tf_op jit(solution)/shard_map/ppermute | solution.py:432
  15.0 6.0 %collective-permute-start.7 = (bf16[4,20,16,128]{3,2,1,0:T(8,128)(2,1)S(1)}, bf16[4,20,16,128]{3,2,1,0:T(8,128)(2,1)S(1)}, u32[]{:S(2)}, u32[]{:S(2)}) collective-permute-start(bf16[4,20,16,128]{3,2,1,0:T(8,128)(2,1)S(1)} %pad_maximum_fusion.near_ref), channel_id=1, source_target_pairs={{0,8},{4,12},{8,0},{12,4},{16,24},{20,28},{24,16},{28,20},{1,9},{5... | collective-permute-start | bytes 983048 | tf_op jit(solution)/shard_map/ppermute | solution.py:416
  20.9 12.1 %copy-start = (f32[8]{0:T(128)S(1)}, f32[8]{0:T(128)}, u32[]{:S(2)}) copy-start(f32[8]{0:T(128)} %cond_ref.1) | copy-start | bytes 100
  20.9 12.1 %copy-start.1 = (f32[8]{0:T(128)S(1)}, f32[8]{0:T(128)}, u32[]{:S(2)}) copy-start(f32[8]{0:T(128)} %alpha_ref.1) | copy-start | bytes 100
  20.9 12.1 %copy-start.2 = (f32[16]{0:T(128)S(1)}, f32[16]{0:T(128)}, u32[]{:S(2)}) copy-start(f32[16]{0:T(128)} %mol_ref.1) | copy-start | bytes 196
  20.9 12.1 %copy-start.3 = (f32[16]{0:T(128)S(1)}, f32[16]{0:T(128)}, u32[]{:S(2)}) copy-start(f32[16]{0:T(128)} %long_ref.1) | copy-start | bytes 196
  20.9 12.0 %collective-permute-start.6 = (bf16[4,4,4,16,128]{4,3,2,1,0:T(8,128)(2,1)S(1)}, bf16[4,4,4,16,128]{4,3,2,1,0:T(8,128)(2,1)S(1)}, u32[]{:S(2)}, u32[]{:S(2)}) collective-permute-start(bf16[4,4,4,16,128]{4,3,2,1,0:T(8,128)(2,1)S(1)} %pad_maximum_fusion.1), channel_id=1, source_target_pairs={{0,8},{4,12},{8,0},{12,4},{16,24},{20,28},{24,16},{28,20},{1,9},{5... | collective-permute-start | bytes 786440 | tf_op jit(solution)/shard_map/ppermute | solution.py:416
  22.4 10.4 %all-to-all-start = ((f32[32,8,128]{2,1,0:T(8,128)}), f32[32,8,128]{2,1,0:T(8,128)S(1)}, u32[]{:S(2)}, u32[]{:S(2)}) async-start(f32[32,8,128]{2,1,0:T(8,128)} %interpolate.1), calls=%async_computation | async-start | bytes 262144 | tf_op jit(solution)/shard_map/all_to_all | solution.py:511
  32.8 2.7 %collective-permute-start.8 = (f32[32,8,128]{2,1,0:T(8,128)S(1)}, f32[32,8,128]{2,1,0:T(8,128)S(1)}, u32[]{:S(2)}, u32[]{:S(2)}) collective-permute-start(f32[32,8,128]{2,1,0:T(8,128)S(1)} %all-to-all-done.own_ref), channel_id=1, source_target_pairs={{0,8},{4,12},{8,0},{12,4},{16,24},{20,28},{24,16},{28,20},{1,9},{5... | collective-permute-start | bytes 393224 | tf_op jit(solution)/shard_map/ppermute | solution.py:416

commit v4 on v3

--- a/solution.py
+++ b/solution.py
@@ -422,7 +422,7 @@
         for shift_y in range(lax.axis_size("gy")):
             if shift_x + shift_y > 0:
                 parts.append(moved(x, shift_x, shift_y))
-    return jnp.stack(parts)
+    return parts
 
 
 def from_depth(x):
@@ -470,9 +470,11 @@
         compiler_params=grant(4),
         name="pack",
     )(in_hbm(tiles), in_hbm(pressure_head), in_hbm(zone_ids), in_hbm(well_cells))
-    near = from_chips(packed)
+    parts = from_chips(packed)
+    near = jnp.stack([part[:tile_count] for part in parts])
     far = moved(near, 1, 0)
-    cells = from_depth(near[:, tile_count:])
+    cells = jnp.stack([part[tile_count:] for part in parts])
+    cells = from_depth(cells)
     cells = jnp.concatenate([cells, moved(cells, 1, 0)])
     cells = cells.reshape((devices,) + cells.shape[2:])
 

time: 46.8 us -> 47.7 us (1.019)
  starting transfers between devices: 11.8 us -> 12.7 us
    all_to_all x1, starting transfers between devices: 2.58 us -> 3.31 us  [field_plan(): lax.all_to_all(fields, AXES, split_axis=0, concat_axis=0, tiled=True)]
  transfers between devices with their start and end apart: 10 -> 10, of which waited for: 6 -> 6; matrix products, arithmetic and copies ran while one was open for 0% -> 1% of each run, Pallas kernels for 12% -> 11%
where the time goes in v4:
time: 47.7 us; the launch traced here: 47.4 us
  waiting for transfers between devices  15.4 us (32%)
  starting transfers between devices  12.7 us (27%)
  blocking collectives  9.84 us (21%)
  Pallas kernels  6.97 us (15%)
  between operations  1.53 us (3%)
  local copies, waits for them, and re-layouts  0.82 us (2%)
    all_to_all x1, blocking collectives, field_plan(): back = lax.all_to_all(back, AXES, split_axis=0, concat_axis=0, tiled=True)  9.84 us
    all_to_all x1, waiting for transfers between devices, field_plan(): lax.all_to_all(fields, AXES, split_axis=0, concat_axis=0, tiled=True)  7.76 us
    ppermute x3, waiting for transfers between devices, from_depth(): parts.append(lax.ppermute(x, 'gz', [(i, i ^ shift) for i in range(count)]))  5.83 us
    ppermute x6, starting transfers between devices, moved(): return lax.ppermute(x, LAYER, pairs)  4.89 us
    ppermute x3, starting transfers between devices, from_depth(): parts.append(lax.ppermute(x, 'gz', [(i, i ^ shift) for i in range(count)]))  4.45 us
    all_to_all x1, starting transfers between devices, field_plan(): lax.all_to_all(fields, AXES, split_axis=0, concat_axis=0, tiled=True)  3.31 us
    pallas_call x1, Pallas kernels, field_plan(): pl.pallas_call(functools.partial(flow_kernel, shape), out_shape=(jax.Shap...  2.42 us
    ppermute x6, waiting for transfers between devices, moved(): return lax.ppermute(x, LAYER, pairs)  1.84 us
  transfers between devices with their start and end apart: 10, of which 6 were waited for; matrix products, arithmetic and copies ran while one was open for 1% of the time, Pallas kernels for 11%

profile of v4, /device:TPU:0, one launch (start us, length us, event | category | flops | bytes accessed | tf_op | source)
XLA Modules:
  0.0 47.4 jit_solution(695184968520470375)
XLA Ops:
  0.6 0.9 %pack.1 = bf16[20,16,128]{2,1,0:T(8,128)(2,1)S(1)} custom-call(bf16[16,16,128]{2,1,0:T(8,128)(2,1)} %bitcast.60, f32[2,8,128]{2,1,0:T(8,128)} %head_s.1, s32[2,8,128]{2,1,0:T(8,128)} %zone_s.1, s32[2,8,128]{2,1,0:T(8,128)} %well_s.1), custom_call_target="tpu_custom_call" | custom-call | tf_op jit(solution)/shard_map/pack/pallas_call | solution.py:462
  1.5 4.0 %collective-permute-start.2 = (bf16[20,16,128]{2,1,0:T(8,128)(2,1)S(1)}, bf16[20,16,128]{2,1,0:T(8,128)(2,1)S(1)}, u32[]{:S(2)}, u32[]{:S(2)}) collective-permute-start(bf16[20,16,128]{2,1,0:T(8,128)(2,1)S(1)} %pack.1), channel_id=1, source_target_pairs={{0,20},{4,16},{8,28},{12,24},{16,4},{20,0},{24,12},{28,8},{1,21},{... | collective-permute-start | bytes 245768 | tf_op jit(solution)/shard_map/ppermute | solution.py:416
  5.5 0.5 %collective-permute-start.1 = (bf16[20,16,128]{2,1,0:T(8,128)(2,1)S(1)}, bf16[20,16,128]{2,1,0:T(8,128)(2,1)S(1)}, u32[]{:S(2)}, u32[]{:S(2)}) collective-permute-start(bf16[20,16,128]{2,1,0:T(8,128)(2,1)S(1)} %pack.1), channel_id=1, source_target_pairs={{0,16},{4,20},{8,24},{12,28},{16,0},{20,4},{24,8},{28,12},{1,17},{... | collective-permute-start | bytes 245768 | tf_op jit(solution)/shard_map/ppermute | solution.py:416
  6.0 0.1 collective-permute-start
  6.8 0.0 copy-start.4
  6.9 0.0 copy-start.5
  6.9 0.0 copy-start.6
  6.9 1.6 %stage.1.weights_ref = bf16[64,128,128]{2,1,0:T(8,128)(2,1)S(1)} custom-call(bf16[64,128,128]{2,1,0:T(8,128)(2,1)} %bitcast.54), custom_call_target="tpu_custom_call" | custom-call | tf_op jit(solution)/shard_map/stage/pallas_call | solution.py:481
  8.5 0.0 copy-done.4
  8.5 0.0 copy-done.5
  8.5 0.0 copy-done.6
  8.6 0.1 add_bitcast_fusion.table_ref
  8.6 0.0 collective-permute-done.2
  8.7 1.3 %collective-permute-done.1 = bf16[20,16,128]{2,1,0:T(8,128)(2,1)S(1)} collective-permute-done((bf16[20,16,128]{2,1,0:T(8,128)(2,1)S(1)}, bf16[20,16,128]{2,1,0:T(8,128)(2,1)S(1)}, u32[]{:S(2)}, u32[]{:S(2)}) %collective-permute-start.1) | collective-permute-done | bytes 81952 | tf_op jit(solution)/shard_map/ppermute | solution.py:416
  10.0 0.5 %collective-permute-done = bf16[20,16,128]{2,1,0:T(8,128)(2,1)S(1)} collective-permute-done((bf16[20,16,128]{2,1,0:T(8,128)(2,1)S(1)}, bf16[20,16,128]{2,1,0:T(8,128)(2,1)S(1)}, u32[]{:S(2)}, u32[]{:S(2)}) %collective-permute-start) | collective-permute-done | bytes 81952 | tf_op jit(solution)/shard_map/ppermute | solution.py:416
  10.5 0.1 collective-permute-start.7
  10.7 2.7 %collective-permute-start.4 = (bf16[4,4,16,128]{3,2,1,0:T(8,128)(2,1)S(1)}, bf16[4,4,16,128]{3,2,1,0:T(8,128)(2,1)S(1)}, u32[]{:S(2)}, u32[]{:S(2)}) collective-permute-start(bf16[4,4,16,128]{3,2,1,0:T(8,128)(2,1)S(1)} %get-tuple-element.9), channel_id=1, source_target_pairs={{0,2},{1,3},{2,0},{3,1},{4,6},{5,7},{6,4},{7,5},{8,10},{9,11},{10,... | collective-permute-start | bytes 196616 | tf_op jit(solution)/shard_map/ppermute | solution.py:432
  13.3 1.6 %collective-permute-start.3 = (bf16[4,4,16,128]{3,2,1,0:T(8,128)(2,1)S(1)}, bf16[4,4,16,128]{3,2,1,0:T(8,128)(2,1)S(1)}, u32[]{:S(2)}, u32[]{:S(2)}) collective-permute-start(bf16[4,4,16,128]{3,2,1,0:T(8,128)(2,1)S(1)} %get-tuple-element.9), channel_id=1, source_target_pairs={{0,1},{1,0},{2,3},{3,2},{4,5},{5,4},{6,7},{7,6},{8,9},{9,8},{10,11... | collective-permute-start | bytes 196616 | tf_op jit(solution)/shard_map/ppermute | solution.py:432
  14.9 0.2 collective-permute-start.5
  15.1 2.4 %collective-permute-done.4 = bf16[4,4,16,128]{3,2,1,0:T(8,128)(2,1)S(1)} collective-permute-done((bf16[4,4,16,128]{3,2,1,0:T(8,128)(2,1)S(1)}, bf16[4,4,16,128]{3,2,1,0:T(8,128)(2,1)S(1)}, u32[]{:S(2)}, u32[]{:S(2)}) %collective-permute-start.4) | collective-permute-done | bytes 65568 | tf_op jit(solution)/shard_map/ppermute | solution.py:432
  17.5 0.4 collective-permute-done.3
  17.8 3.1 %collective-permute-done.5 = bf16[4,4,16,128]{3,2,1,0:T(8,128)(2,1)S(1)} collective-permute-done((bf16[4,4,16,128]{3,2,1,0:T(8,128)(2,1)S(1)}, bf16[4,4,16,128]{3,2,1,0:T(8,128)(2,1)S(1)}, u32[]{:S(2)}, u32[]{:S(2)}) %collective-permute-start.5) | collective-permute-done | bytes 65568 | tf_op jit(solution)/shard_map/ppermute | solution.py:432
  21.0 0.0 copy-start
  21.0 0.0 copy-start.1
  21.0 0.0 copy-start.2
  21.0 0.0 copy-start.3
  21.0 0.1 collective-permute-start.6
  21.1 0.0 collective-permute-done.7.far_ref
  21.1 1.4 %interpolate.1 = f32[32,8,128]{2,1,0:T(8,128)} custom-call(s32[1,128]{1,0:T(1,128)S(1)} %add_bitcast_fusion.table_ref, bf16[4,16,16,128]{3,2,1,0:T(8,128)(2,1)S(1)} %pad_maximum_fusion.1.near_ref, bf16[4,16,16,128]{3,2,1,0:T(8,128)(2,1)S(1)} %collective-permute-done.7.far_ref, bf16[64,128,128]{2,1,0:T(8,128)(2,1)S(1)} %stage.1.weights_ref), custom_call_target="tpu_custom_call" | custom-call | tf_op jit(solution)/shard_map/interpolate/pallas_call | solution.py:501
  22.5 3.3 %all-to-all-start = ((f32[32,8,128]{2,1,0:T(8,128)}), f32[32,8,128]{2,1,0:T(8,128)S(1)}, u32[]{:S(2)}, u32[]{:S(2)}) async-start(f32[32,8,128]{2,1,0:T(8,128)} %interpolate.1), calls=%async_computation | async-start | bytes 262144 | tf_op jit(solution)/shard_map/all_to_all | solution.py:513
  25.8 7.8 %all-to-all-done.own_ref = f32[32,8,128]{2,1,0:T(8,128)S(1)} async-done(((f32[32,8,128]{2,1,0:T(8,128)}), f32[32,8,128]{2,1,0:T(8,128)S(1)}, u32[]{:S(2)}, u32[]{:S(2)}) %all-to-all-start) | async-done | bytes 131104 | tf_op jit(solution)/shard_map/all_to_all | solution.py:513
  33.6 0.1 collective-permute-start.8
  33.7 0.0 collective-permute-done.6
  33.8 0.0 copy-done
  33.8 0.0 copy-done.1
  33.8 0.0 copy-done.2
  33.8 0.0 copy-done.3
  33.8 2.4 %flow.1 = (f32[3,8,2,4,8,128]{5,4,3,2,1,0:T(8,128)S(1)}, f32[8,128]{1,0:T(8,128)S(1)}, f32[2,8,128]{2,1,0:T(8,128)}) custom-call(f32[8]{0:T(128)S(1)} %copy-done, f32[8]{0:T(128)S(1)} %copy-done.1, f32[16]{0:T(128)S(1)} %copy-done.2, f32[16]{0:T(128)S(1)} %copy-done.3, bf16[32,4,16,128]{3,2,1,0:T(8,128)(2,1)S(1)} %bitcast.53), custom_call_target="tpu_custom_call" | custom-call | tf_op jit(solution)/shard_map/flow/pallas_call | solution.py:517
  36.3 0.0 collective-permute-done.8.other_ref
  36.3 0.7 %solve.1 = f32[32,8,128]{2,1,0:T(8,128)S(1)} custom-call(f32[32,8,128]{2,1,0:T(8,128)S(1)} %all-to-all-done.own_ref, f32[32,8,128]{2,1,0:T(8,128)S(1)} %collective-permute-done.8.other_ref, f32[3,8,2,4,8,128]{5,4,3,2,1,0:T(8,128)S(1)} %get-tuple-element.6.face_ref, f32[8,128]{1,0:T(8,128)S(1)} %get-tuple-element.7.edge_ref), custom_call_target="tpu_custom_call" | custom-call | tf_op jit(solution)/shard_map/solve/pallas_call | solution.py:531
  36.9 9.8 %all_to_all.10 = f32[32,8,128]{2,1,0:T(8,128)S(1)} all-to-all(f32[32,8,128]{2,1,0:T(8,128)S(1)} %solve.1), channel_id=1, replica_groups=mesh['gx'=4,'gy'=2,'gz'=4] {'gx','gy','gz'}, dimensions={0} | all-to-all | bytes 262144 | tf_op jit(solution)/shard_map/all_to_all | solution.py:540
  46.8 0.7 %copy.15 = f32[2,8,2,8,128]{4,3,2,1,0:T(8,128)} copy(f32[2,8,2,8,128]{4,3,1,2,0:T(8,128)S(1)} %bitcast.55) | data formatting | bytes 262144 | tf_op jit(solution)/shard_map/transpose | solution.py:542
  (17 shorter events, 0.2 us)
Async XLA Ops:
  1.5 7.1 %collective-permute-start.2 = (bf16[20,16,128]{2,1,0:T(8,128)(2,1)S(1)}, bf16[20,16,128]{2,1,0:T(8,128)(2,1)S(1)}, u32[]{:S(2)}, u32[]{:S(2)}) collective-permute-start(bf16[20,16,128]{2,1,0:T(8,128)(2,1)S(1)} %pack.1), channel_id=1, source_target_pairs={{0,20},{4,16},{8,28},{12,24},{16,4},{20,0},{24,12},{28,8},{1,21},{... | collective-permute-start | bytes 245768 | tf_op jit(solution)/shard_map/ppermute | solution.py:416
  5.5 4.4 %collective-permute-start.1 = (bf16[20,16,128]{2,1,0:T(8,128)(2,1)S(1)}, bf16[20,16,128]{2,1,0:T(8,128)(2,1)S(1)}, u32[]{:S(2)}, u32[]{:S(2)}) collective-permute-start(bf16[20,16,128]{2,1,0:T(8,128)(2,1)S(1)} %pack.1), channel_id=1, source_target_pairs={{0,16},{4,20},{8,24},{12,28},{16,0},{20,4},{24,8},{28,12},{1,17},{... | collective-permute-start | bytes 245768 | tf_op jit(solution)/shard_map/ppermute | solution.py:416
  6.0 4.4 %collective-permute-start = (bf16[20,16,128]{2,1,0:T(8,128)(2,1)S(1)}, bf16[20,16,128]{2,1,0:T(8,128)(2,1)S(1)}, u32[]{:S(2)}, u32[]{:S(2)}) collective-permute-start(bf16[20,16,128]{2,1,0:T(8,128)(2,1)S(1)} %pack.1), channel_id=1, source_target_pairs={{0,4},{4,0},{8,12},{12,8},{16,20},{20,16},{24,28},{28,24},{1,5},{5... | collective-permute-start | bytes 245768 | tf_op jit(solution)/shard_map/ppermute | solution.py:416
  6.8 1.7 %copy-start.4 = (s32[1,1,1,64]{3,2,1,0:T(1,128)S(1)}, s32[1,1,1,64]{3,2,1,0:T(1,128)}, u32[]{:S(2)}) copy-start(s32[1,1,1,64]{3,2,1,0:T(1,128)} %param.22) | copy-start | bytes 772
  6.9 1.7 %copy-start.5 = (s32[1,1,1,64]{3,2,1,0:T(1,128)S(1)}, s32[1,1,1,64]{3,2,1,0:T(1,128)}, u32[]{:S(2)}) copy-start(s32[1,1,1,64]{3,2,1,0:T(1,128)} %param.24) | copy-start | bytes 772
  6.9 1.7 %copy-start.6 = (s32[1,1,1,64,1]{3,4,2,1,0:T(1,128)S(1)}, s32[1,1,1,64,1]{3,4,2,1,0:T(1,128)}, u32[]{:S(2)}) copy-start(s32[1,1,1,64,1]{3,4,2,1,0:T(1,128)} %param.23) | copy-start | bytes 772
  10.5 10.6 %collective-permute-start.7 = (bf16[4,16,16,128]{3,2,1,0:T(8,128)(2,1)S(1)}, bf16[4,16,16,128]{3,2,1,0:T(8,128)(2,1)S(1)}, u32[]{:S(2)}, u32[]{:S(2)}) collective-permute-start(bf16[4,16,16,128]{3,2,1,0:T(8,128)(2,1)S(1)} %pad_maximum_fusion.1.near_ref), channel_id=1, source_target_pairs={{0,8},{4,12},{8,0},{12,4},{16,24},{20,28},{24,16},{28,20},{1,9},{5... | collective-permute-start | bytes 786440 | tf_op jit(solution)/shard_map/ppermute | solution.py:416
  10.7 6.8 %collective-permute-start.4 = (bf16[4,4,16,128]{3,2,1,0:T(8,128)(2,1)S(1)}, bf16[4,4,16,128]{3,2,1,0:T(8,128)(2,1)S(1)}, u32[]{:S(2)}, u32[]{:S(2)}) collective-permute-start(bf16[4,4,16,128]{3,2,1,0:T(8,128)(2,1)S(1)} %get-tuple-element.9), channel_id=1, source_target_pairs={{0,2},{1,3},{2,0},{3,1},{4,6},{5,7},{6,4},{7,5},{8,10},{9,11},{10,... | collective-permute-start | bytes 196616 | tf_op jit(solution)/shard_map/ppermute | solution.py:432
  13.3 4.5 %collective-permute-start.3 = (bf16[4,4,16,128]{3,2,1,0:T(8,128)(2,1)S(1)}, bf16[4,4,16,128]{3,2,1,0:T(8,128)(2,1)S(1)}, u32[]{:S(2)}, u32[]{:S(2)}) collective-permute-start(bf16[4,4,16,128]{3,2,1,0:T(8,128)(2,1)S(1)} %get-tuple-element.9), channel_id=1, source_target_pairs={{0,1},{1,0},{2,3},{3,2},{4,5},{5,4},{6,7},{7,6},{8,9},{9,8},{10,11... | collective-permute-start | bytes 196616 | tf_op jit(solution)/shard_map/ppermute | solution.py:432
  14.9 6.1 %collective-permute-start.5 = (bf16[4,4,16,128]{3,2,1,0:T(8,128)(2,1)S(1)}, bf16[4,4,16,128]{3,2,1,0:T(8,128)(2,1)S(1)}, u32[]{:S(2)}, u32[]{:S(2)}) collective-permute-start(bf16[4,4,16,128]{3,2,1,0:T(8,128)(2,1)S(1)} %get-tuple-element.9), channel_id=1, source_target_pairs={{0,3},{1,2},{2,1},{3,0},{4,7},{5,6},{6,5},{7,4},{8,11},{9,10},{10,... | collective-permute-start | bytes 196616 | tf_op jit(solution)/shard_map/ppermute | solution.py:432
  21.0 12.8 %copy-start = (f32[8]{0:T(128)S(1)}, f32[8]{0:T(128)}, u32[]{:S(2)}) copy-start(f32[8]{0:T(128)} %cond_ref.1) | copy-start | bytes 100
  21.0 12.8 %copy-start.1 = (f32[8]{0:T(128)S(1)}, f32[8]{0:T(128)}, u32[]{:S(2)}) copy-start(f32[8]{0:T(128)} %alpha_ref.1) | copy-start | bytes 100
  21.0 12.8 %copy-start.2 = (f32[16]{0:T(128)S(1)}, f32[16]{0:T(128)}, u32[]{:S(2)}) copy-start(f32[16]{0:T(128)} %mol_ref.1) | copy-start | bytes 196
  21.0 12.8 %copy-start.3 = (f32[16]{0:T(128)S(1)}, f32[16]{0:T(128)}, u32[]{:S(2)}) copy-start(f32[16]{0:T(128)} %long_ref.1) | copy-start | bytes 196
  21.0 12.7 %collective-permute-start.6 = (bf16[4,4,4,16,128]{4,3,2,1,0:T(8,128)(2,1)S(1)}, bf16[4,4,4,16,128]{4,3,2,1,0:T(8,128)(2,1)S(1)}, u32[]{:S(2)}, u32[]{:S(2)}) collective-permute-start(bf16[4,4,4,16,128]{4,3,2,1,0:T(8,128)(2,1)S(1)} %pad_maximum_fusion), channel_id=1, source_target_pairs={{0,8},{4,12},{8,0},{12,4},{16,24},{20,28},{24,16},{28,20},{1,9},{5... | collective-permute-start | bytes 786440 | tf_op jit(solution)/shard_map/ppermute | solution.py:416
  22.5 11.1 %all-to-all-start = ((f32[32,8,128]{2,1,0:T(8,128)}), f32[32,8,128]{2,1,0:T(8,128)S(1)}, u32[]{:S(2)}, u32[]{:S(2)}) async-start(f32[32,8,128]{2,1,0:T(8,128)} %interpolate.1), calls=%async_computation | async-start | bytes 262144 | tf_op jit(solution)/shard_map/all_to_all | solution.py:513
  33.6 2.7 %collective-permute-start.8 = (f32[32,8,128]{2,1,0:T(8,128)S(1)}, f32[32,8,128]{2,1,0:T(8,128)S(1)}, u32[]{:S(2)}, u32[]{:S(2)}) collective-permute-start(f32[32,8,128]{2,1,0:T(8,128)S(1)} %all-to-all-done.own_ref), channel_id=1, source_target_pairs={{0,8},{4,12},{8,0},{12,4},{16,24},{20,28},{24,16},{28,20},{1,9},{5... | collective-permute-start | bytes 393224 | tf_op jit(solution)/shard_map/ppermute | solution.py:416
